TPU v7x, 256 devices: a whole 4x4x8 slice. The times are simulated.
256 devices in a mesh: bank: 128 (over y, z, x), sub: 2 (over core).
Axes of the slice: x: 4, y: 4, z: 8, core: 2. Of those that a mesh axis runs over, the one named last changes fastest.
Arguments:
- embeddings: bfloat16 [786432, 1024], P(('bank', 'sub'))
- pivots: int32 [2, 256], replicated, may hold values from 0 to 786431, as said below
Outputs:
- basis: float32 [786432, 512], P(('bank', 'sub'))
- triangle: float32 [512, 512], replicated
Inputs may be any that keep to these rules, and one draw needn't show every extreme that they name: All 512 entries are distinct molecules. Molecule g lies on device g // 3072 of bank+sub (bank slowest). Each device holds at most 1 pivots of each block step, and some device holds exactly 1.
All inputs are finite; a program needn't handle non-finite values.
Results may differ from a plain program's by a relative error of at most 0.0003.
Values may be sent and summed in bfloat16 or wider, within the bound.
A program may use at most 64 MiB of HBM per device.

v0:
```python
import jax
import jax.numpy as jnp
from jax import lax
from jax.sharding import PartitionSpec as P

P_SIZE = 256


def lower_inverse(factor):
    identity = jnp.eye(factor.shape[0], dtype=factor.dtype)
    return lax.linalg.triangular_solve(factor, identity, left_side=True, lower=True)


def times_transposed(left, right, exact):
    if exact:
        return lax.dot_general(
            left,
            right,
            (((1,), (1,)), ((), ())),
            precision=lax.Precision.HIGHEST,
            preferred_element_type=jnp.float32,
        )
    return lax.dot_general(
        left, right, (((1,), (1,)), ((), ())), preferred_element_type=jnp.float32
    )


def per_device(embeddings, pivots):
    device_count = lax.axis_size(("bank", "sub"))
    my_index = lax.axis_index(("bank", "sub"))
    row_count = embeddings.shape[0]
    start_row = my_index * row_count
    flat_list = pivots.reshape(-1)
    present = (flat_list >= start_row) & (flat_list < start_row + row_count)
    local_index = jnp.clip(flat_list - start_row, 0, row_count - 1)
    picked = jnp.take(embeddings, local_index, axis=0).astype(jnp.float32) * present[
        :, None
    ].astype(jnp.float32)
    chosen = lax.psum(picked, ("bank", "sub")).astype(jnp.bfloat16)
    norms = jnp.einsum("rd,rd->r", embeddings, embeddings, preferred_element_type=jnp.float32)
    chosen_norms = jnp.einsum("rd,rd->r", chosen, chosen, preferred_element_type=jnp.float32)
    dots = times_transposed(embeddings, chosen, False)
    similar = dots / (norms[:, None] + chosen_norms[None, :] - dots)
    block_dots = times_transposed(chosen, chosen, False)
    block = block_dots / (chosen_norms[:, None] + chosen_norms[None, :] - block_dots)
    first_inverse = lower_inverse(jnp.linalg.cholesky(block[:P_SIZE, :P_SIZE]))
    first_factor = times_transposed(similar[:, :P_SIZE], first_inverse, True)
    pivot_first = times_transposed(block[P_SIZE:, :P_SIZE], first_inverse, True)
    second_cols = similar[:, P_SIZE:] - times_transposed(first_factor, pivot_first, True)
    second_block = block[P_SIZE:, P_SIZE:] - times_transposed(pivot_first, pivot_first, True)
    second_inverse = lower_inverse(jnp.linalg.cholesky(second_block))
    second_factor = times_transposed(second_cols, second_inverse, True)
    factor = jnp.concatenate([first_factor, second_factor], axis=1)
    total_rows = row_count * device_count
    local_gram = (
        lax.dot_general(
            factor,
            factor,
            (((0,), (0,)), ((), ())),
            precision=lax.Precision.HIGHEST,
            preferred_element_type=jnp.float32,
        )
        / total_rows
    )
    gram = lax.psum(local_gram, ("bank", "sub"))
    lower_root = jnp.linalg.cholesky(gram)
    basis = times_transposed(factor, lower_inverse(lower_root), True)
    return (basis, lower_root.T)


def solution(mesh):
    in_specs = (P(("bank", "sub"), None), P())
    out_specs = (P(("bank", "sub"), None), P())
    return jax.shard_map(
        per_device, mesh=mesh, in_specs=in_specs, out_specs=out_specs, check_vma=False
    )
```

profile of v0, /device:TPU:1, one launch (start us, length us, event | category | flops | bytes accessed | tf_op | source)
XLA Modules:
  0.0 710.3 jit_solution(15264910173335622265)
XLA Ops:
  8.7 4.1 fusion
  12.8 6.3 gather_fusion
  19.5 90.1 %all-reduce.6 = bf16[512,1024]{1,0:T(8,128)(2,1)S(1)} all-reduce(f32[512,1024]{1,0:T(8,128)S(1)} %convert_multiply_fusion.2), channel_id=1, replica_groups=mesh['bank'=128,'sub'=2] {'bank','sub'}, use_global_device_ids=true, to_apply=%region_0.1 | all-reduce | flops 524288 | bytes 3145728 | tf_op jit(solution)/shard_map/psum | solution.py:39
  110.9 11.7 %cholesky.357 = f32[128,128]{1,0:T(8,128)S(1)} custom-call(f32[128,128]{1,0:T(8,128)S(1)} %cholesky.407), custom_call_target="Cholesky" | custom-call | tf_op jit(solution)/shard_map/jit(cholesky)/cholesky | solution.py:46
  122.6 9.8 %custom-call.43 = f32[1,128,128]{1,2,0:T(8,128)S(1)} custom-call(f32[1,128,128]{2,1,0:T(8,128)S(1)} %get-tuple-element.80), custom_call_target="InvertDiagBlocksLowerTriangular" | custom-call | tf_op jit(solution)/shard_map/jit(cholesky)/cholesky/custom-call.1 | solution.py:46
  133.0 11.7 %cholesky.367 = f32[128,128]{1,0:T(8,128)S(1)} custom-call(f32[128,128]{1,0:T(8,128)S(1)} %convolution_subtract_fusion.10), custom_call_target="Cholesky" | custom-call | tf_op jit(solution)/shard_map/jit(cholesky)/cholesky | solution.py:46
  146.7 3.8 while.6
  150.5 20.1 %custom-call.44 = f32[2,128,128]{1,2,0:T(8,128)S(1)} custom-call(f32[2,128,128]{2,1,0:T(8,128)S(1)} %get-tuple-element.27), custom_call_target="InvertDiagBlocksLowerTriangular" | custom-call | tf_op jit(solution)/shard_map/triangular_solve/custom-call.9 | solution.py:11
  173.4 11.7 %cholesky.384 = f32[128,128]{1,0:T(8,128)S(1)} custom-call(f32[128,128]{1,0:T(8,128)S(1)} %cholesky.410), custom_call_target="Cholesky" | custom-call | tf_op jit(solution)/shard_map/jit(cholesky)/cholesky | solution.py:51
  185.2 9.8 %custom-call.45 = f32[1,128,128]{1,2,0:T(8,128)S(1)} custom-call(f32[1,128,128]{2,1,0:T(8,128)S(1)} %get-tuple-element.76), custom_call_target="InvertDiagBlocksLowerTriangular" | custom-call | tf_op jit(solution)/shard_map/jit(cholesky)/cholesky/custom-call.1 | solution.py:51
  195.5 11.7 %cholesky.394 = f32[128,128]{1,0:T(8,128)S(1)} custom-call(f32[128,128]{1,0:T(8,128)S(1)} %convolution_subtract_fusion.9), custom_call_target="Cholesky" | custom-call | tf_op jit(solution)/shard_map/jit(cholesky)/cholesky | solution.py:51
  209.8 3.8 while.7
  213.5 19.9 %custom-call.46 = f32[2,128,128]{1,2,0:T(8,128)S(1)} custom-call(f32[2,128,128]{2,1,0:T(8,128)S(1)} %get-tuple-element.28), custom_call_target="InvertDiagBlocksLowerTriangular" | custom-call | tf_op jit(solution)/shard_map/triangular_solve/custom-call.9 | solution.py:11
  234.3 5.7 subtract_divide_fusion
  240.1 3.0 fusion.3
  243.1 3.2 convolution_subtract_fusion
  246.3 3.0 fusion.30
  251.0 11.9 %fusion.17 = f32[512,512]{0,1:T(8,128)} fusion(f32[3072,256]{0,1:T(8,128)S(1)} %fusion.30, f32[3072,256]{0,1:T(8,128)S(1)} %fusion.3), kind=kOutput, calls=%fused_computation.50 | convolution fusion | flops 9665511424 | bytes 7340032 | tf_op jit(solution)/shard_map/dot_general | solution.py:56
  264.9 252.2 %all-reduce.5.cloned.1.call-done = f32[512,512]{0,1:T(8,128)} async-done(((f32[512,512]{0,1:T(8,128)}), f32[512,512]{0,1:T(8,128)}) %all-reduce.5.cloned.1.call-update) | async-done | bytes 1048592 | tf_op jit(solution)/shard_map/psum | solution.py:65
  522.4 11.7 %cholesky.167 = f32[128,128]{1,0:T(8,128)S(1)} custom-call(f32[128,128]{1,0:T(8,128)S(1)} %cholesky.413), custom_call_target="Cholesky" | custom-call | tf_op jit(solution)/shard_map/jit(cholesky)/cholesky | solution.py:66
  535.3 9.8 %custom-call.35 = f32[1,128,128]{1,2,0:T(8,128)S(1)} custom-call(f32[1,128,128]{2,1,0:T(8,128)S(1)} %get-tuple-element.72), custom_call_target="InvertDiagBlocksLowerTriangular" | custom-call | tf_op jit(solution)/shard_map/jit(cholesky)/cholesky | solution.py:66
  548.3 11.7 %cholesky.190 = f32[128,128]{1,0:T(8,128)S(1)} custom-call(f32[128,128]{1,0:T(8,128)S(1)} %cholesky.417), custom_call_target="Cholesky" | custom-call | tf_op jit(solution)/shard_map/jit(cholesky)/cholesky | solution.py:66
  562.0 9.9 %custom-call.36 = f32[1,128,128]{1,2,0:T(8,128)S(1)} custom-call(f32[1,128,128]{2,1,0:T(8,128)S(1)} %get-tuple-element.69), custom_call_target="InvertDiagBlocksLowerTriangular" | custom-call | tf_op jit(solution)/shard_map/jit(cholesky)/cholesky | solution.py:66
  574.3 11.7 %cholesky.294 = f32[128,128]{1,0:T(8,128)S(1)} custom-call(f32[128,128]{1,0:T(8,128)S(1)} %cholesky.422), custom_call_target="Cholesky" | custom-call | tf_op jit(solution)/shard_map/jit(cholesky)/cholesky | solution.py:66
  587.4 9.8 %custom-call.47 = f32[1,128,128]{1,2,0:T(8,128)S(1)} custom-call(f32[1,128,128]{2,1,0:T(8,128)S(1)} %get-tuple-element.66), custom_call_target="InvertDiagBlocksLowerTriangular" | custom-call | tf_op jit(solution)/shard_map/jit(cholesky)/cholesky/custom-call.1 | solution.py:66
  599.4 11.9 %cholesky.307 = f32[128,128]{1,0:T(8,128)S(1)} custom-call(f32[128,128]{1,0:T(8,128)S(1)} %convolution_subtract_fusion.11), custom_call_target="Cholesky" | custom-call | tf_op jit(solution)/shard_map/jit(cholesky)/cholesky | solution.py:66
  618.1 13.8 %while.5 = (s32[]{:T(128)}, f32[512,512]{1,0:T(8,128)}, s32[4,2]{0,1:T(2,128)S(1)}, f32[4,128,128]{2,1,0:T(8,128)}, s32[]{:T(128)}) while((s32[]{:T(128)}, f32[512,512]{1,0:T(8,128)}, s32[4,2]{0,1:T(2,128)S(1)}, f32[4,128,128]{2,1,0:T(8,128)}, s32[]{:T(128)}) %tuple.78), condition=%wide.while_cond.1, body=%wide.while_body.1.sunk | while | flops 2 | bytes 132705 | solution.py:11
  618.7 2.8 bitcast_dynamic-update-slice_fusion.6
  622.2 2.8 bitcast_dynamic-update-slice_fusion.6
  625.7 2.8 bitcast_dynamic-update-slice_fusion.6
  631.9 40.1 %custom-call.37 = f32[4,128,128]{1,2,0:T(8,128)S(1)} custom-call(f32[4,128,128]{2,1,0:T(8,128)} %get-tuple-element.20), custom_call_target="InvertDiagBlocksLowerTriangular" | custom-call | tf_op jit(solution)/shard_map/triangular_solve | solution.py:11
  679.1 21.6 %fusion.1 = f32[3072,512]{1,0:T(8,128)} fusion(f32[3072,256]{0,1:T(8,128)S(1)} %copy-done.1, f32[3072,256]{0,1:T(8,128)S(1)} %fusion.3, f32[128,512]{1,0:T(8,128)S(1)} %fusion.50, f32[128,512]{1,0:T(8,128)S(1)} %fusion.51, f32[128,512]{1,0:T(8,128)S(1)} %fusion.53, f32[128,512]{1,0:T(8,128)S(1)} %fusion.37), kind=kOutput, calls=%fused_computation.11 | convolution fusion | flops 9666035712 | bytes 13631488 | tf_op jit(solution)/shard_map/dot_general | solution.py:16
  (117 shorter events, 57.6 us)
Async XLA Ops:
  7.2 509.9 %all-reduce.5.cloned.1.call-start = ((), (), s32[]{:S(2)}) async-start(), calls=%async_computation | async-start | bytes 2097152 | tf_op jit(solution)/shard_map/psum | solution.py:65
  7.2 163.7 %copy-start.3 = (f32[256,256]{1,0:T(8,128)}, f32[256,256]{1,0:T(8,128)S(1)}, u32[]{:S(2)}) copy-start(f32[256,256]{1,0:T(8,128)S(1)} %fusion.36) | copy-start | bytes 786436
  171.2 62.2 %copy-start.4 = (f32[256,256]{1,0:T(8,128)S(1)}, f32[256,256]{1,0:T(8,128)}, u32[]{:S(2)}) copy-start(f32[256,256]{1,0:T(8,128)} %copy-done.3) | copy-start | bytes 786436
  171.5 0.7 copy-start.5
  234.3 5.8 copy-start.6
  249.3 1.7 copy-start
  521.4 1.0 copy-start.2
  672.0 7.1 copy-start.1
Sparse Core Ops, SparseCore 0:
  263.1 253.9 all-reduce.4
where the time goes:
time: 716 us; the launch traced here: 710 us
  waiting for transfers between devices  252 us (35%)
  other arithmetic  243 us (34%)
  blocking collectives  90.1 us (13%)
  matrix products  67.7 us (9%)
  local copies, waits for them, and re-layouts  37.6 us (5%)
  between operations  19.8 us (3%)
    psum x1, waiting for transfers between devices, per_device(): gram = lax.psum(local_gram, ('bank', 'sub'))  252 us
    psum x1, blocking collectives, per_device(): chosen = lax.psum(picked, ('bank', 'sub')).astype(jnp.bfloat16)  90.1 us
    another operation x15, other arithmetic, per_device(): lower_root = jnp.linalg.cholesky(gram)  81.3 us
    another operation x7, other arithmetic, lower_inverse(): lax.linalg.triangular_solve(factor, identity, left_side=True, lower=True)  80.1 us
    another operation x7, other arithmetic, per_device(): second_inverse = lower_inverse(jnp.linalg.cholesky(second_block))  34.6 us
    another operation x6, other arithmetic, per_device(): first_inverse = lower_inverse(jnp.linalg.cholesky(block[:P_SIZE, :P_SIZE]))  34 us
    dot_general x6, matrix products, times_transposed(): lax.dot_general(left, right, (((1,), (1,)), ((), ())), precision=lax.Prec...  31.8 us
  transfers between devices with their start and end apart: 1, of which 1 were waited for; matrix products, arithmetic and copies ran while one was open for 0% of the time, Pallas kernels for 0%

commit v1 on v0

v1 whole, which is shorter than its diff:
```python
import jax
import jax.numpy as jnp
from jax import lax
from jax.experimental import pallas as pl
from jax.experimental.pallas import tpu as pltpu
from jax.sharding import PartitionSpec as P

HI = lax.Precision.HIGHEST
F32 = jnp.float32
BF16 = jnp.bfloat16
P_SIZE = 256
NX, NY, NZ = 4, 4, 8
NB = 64
TILE = 512
UPPER = [(i, j) for i in range(4) for j in range(i, 4)]
MESH = pl.DeviceIdType.MESH


def dot(a, b, dims, precision=None):
    return lax.dot_general(a, b, ((dims[:1], dims[1:]), ((), ())), precision=precision, preferred_element_type=F32)


def base_block(rows):
    count = NB // 8
    rows = list(rows)
    sub = lax.broadcasted_iota(jnp.int32, (8, 128), 0)
    full = lambda v: jnp.broadcast_to(v, (8, 128))
    out = []
    for k in range(count):
        cols = [[full(rows[t][:, 8 * k + c : 8 * k + c + 1]) for c in range(8)] for t in range(k, count)]
        scale = jnp.zeros((8, 128), F32)
        for c in range(8):
            pivot = full(cols[0][c][c : c + 1, :])
            pivot_row = full(rows[k][c : c + 1, :])
            ahead = [full(cols[0][e][c : c + 1, :]) for e in range(c + 1, 8)]
            inverse = 1.0 / pivot
            scale = jnp.where(sub == c, pivot, scale)
            for t in range(k, count):
                mult = cols[t - k][c] * inverse
                if t == k:
                    mult = jnp.where(sub > c, mult, 0.0)
                rows[t] = rows[t] - mult * pivot_row
                for e in range(c + 1, 8):
                    cols[t - k][e] = cols[t - k][e] - mult * ahead[e - c - 1]
        out.append(rows[k] * lax.rsqrt(scale))
    return out


def cholesky_inverse(w_ref, diag_ref):
    n = w_ref.shape[0]
    lane = lax.broadcasted_iota(jnp.int32, (8, 128), 1)
    sub = lax.broadcasted_iota(jnp.int32, (8, 128), 0)
    for k in range(n // NB):
        r0 = k * NB
        left = (r0 // 128) * 128
        rows = []
        for t in range(NB // 8):
            block = w_ref[r0 + 8 * t : r0 + 8 * t + 8, left : left + 128]
            if r0 % 128:
                block = pltpu.roll(block, 64, 1)
            rows.append(jnp.where(lane < 64, block, jnp.where(lane - 64 == sub + 8 * t, 1.0, 0.0)))
        both = jnp.concatenate(base_block(rows), axis=0)
        diag_ref[k] = both
        wide = w_ref[r0 : r0 + NB, :]
        col = lax.broadcasted_iota(jnp.int32, (NB, n), 1)
        row = lax.broadcasted_iota(jnp.int32, (NB, n), 0)
        wide = jnp.where((col >= r0) & (col < r0 + NB), jnp.where(col - r0 == row, 1.0, 0.0), wide)
        strip = dot(both[:, 64:], wide, (1, 0), HI)
        w_ref[r0 : r0 + NB, :] = strip
        if r0 + NB < n:
            rest = n - r0 - NB
            update = dot(strip[:, r0 + NB :], strip, (0, 0), HI)
            current = w_ref[r0 + NB :, :]
            col = lax.broadcasted_iota(jnp.int32, (rest, n), 1)
            current = jnp.where((col >= r0) & (col < r0 + NB), 0.0, current)
            w_ref[r0 + NB :, :] = current - update


def lower_blocks(w):
    n = w.shape[0]
    row = lax.broadcasted_iota(jnp.int32, (n, n), 0)
    col = lax.broadcasted_iota(jnp.int32, (n, n), 1)
    return jnp.where(row >= col, w, 0.0)


def coords():
    bank = lax.axis_index("bank")
    core = lax.axis_index("sub")
    x = lax.rem(bank, NX)
    z = lax.rem(bank // NX, NZ)
    y = bank // (NX * NZ)
    return x, y, z, core


def bank_of(x, y, z):
    return (y * NZ + z) * NX + x


def greet(peers):
    barrier = pltpu.get_barrier_semaphore()
    for peer in peers:
        pl.semaphore_signal(barrier, inc=1, device_id=peer, device_id_type=MESH)
    pl.semaphore_wait(barrier, len(peers))


def axis_peers(x, y, z, core):
    along_x = [(bank_of(lax.rem(x + o, NX), y, z), core) for o in range(1, NX)]
    along_y = [(bank_of(x, lax.rem(y + o, NY), z), core) for o in range(1, NY)]
    along_z = [(bank_of(x, y, lax.rem(z + o, NZ)), core) for o in range(1, NZ)]
    return along_x, along_y, along_z


def gather_kernel(mine_ref, out_ref, send, recv):
    x, y, z, core = coords()
    other = (lax.axis_index("bank"), 1 - core)
    along_x, along_y, along_z = axis_peers(x, y, z, core)
    half = NX * NY * NZ
    slot_a = core * half + (y * NZ + z) * NX + x
    slot_b = core * half + (x * NZ + z) * NY + y
    local = pltpu.make_async_copy(mine_ref.at[0], out_ref.at[0, slot_a], send.at[0])
    local_b = pltpu.make_async_copy(mine_ref.at[1], out_ref.at[1, slot_b], send.at[1])
    local.start()
    local_b.start()
    greet([other] + along_x + along_y + along_z)
    local.wait()
    local_b.wait()
    count = [2]

    def push(step, start, size, peers):
        copies = []
        for peer in peers:
            i = count[0]
            count[0] += 1
            part = out_ref.at[step, pl.ds(start, size)]
            copy = pltpu.make_async_remote_copy(
                src_ref=part, dst_ref=part, send_sem=send.at[i], recv_sem=recv.at[i], device_id=peer, device_id_type=MESH
            )
            copy.start()
            copies.append(copy)
        return copies

    base = core * half
    first_a = push(0, base + (y * NZ + z) * NX + x, 1, along_x)
    first_b = push(1, base + (x * NZ + z) * NY + y, 1, along_y)
    for copy in first_a:
        copy.wait_recv()
    second_a = push(0, base + (y * NZ + z) * NX, NX, along_z)
    for copy in first_b:
        copy.wait_recv()
    second_b = push(1, base + (x * NZ + z) * NY, NY, along_z)
    for copy in second_a:
        copy.wait_recv()
    third_a = push(0, base + y * NZ * NX, NZ * NX, along_y)
    for copy in second_b:
        copy.wait_recv()
    third_b = push(1, base + x * NZ * NY, NZ * NY, along_x)
    for copy in third_a:
        copy.wait_recv()
    last_a = push(0, base, half, [other])
    for copy in third_b:
        copy.wait_recv()
    last_b = push(1, base, half, [other])
    for copy in last_a + last_b:
        copy.wait_recv()
    for copy in first_a + first_b + second_a + second_b + third_a + third_b + last_a + last_b:
        copy.wait_send()


def gather_rows(mine):
    copies = 2 + 2 * (3 + 7 + 3 + 1)
    return pl.pallas_call(
        gather_kernel,
        out_shape=jax.ShapeDtypeStruct((2, 256, 8, 128), BF16),
        in_specs=[pl.BlockSpec(memory_space=pltpu.VMEM)],
        out_specs=pl.BlockSpec(memory_space=pltpu.VMEM),
        scratch_shapes=[pltpu.SemaphoreType.DMA((copies,)), pltpu.SemaphoreType.DMA((copies,))],
        compiler_params=pltpu.CompilerParams(collective_id=0, has_side_effects=True),
        name="gather_rows",
    )(mine)


def factor_kernel(targets_ref, rows_ref, emb_ref, factor_ref, gram_ref, wide_ref, chosen_ref, w_ref, inv_ref, diag_ref, norm_ref):
    step = pl.program_id(0)

    @pl.when(step == 0)
    def _():
        for s in range(2):
            slot = lax.broadcasted_iota(jnp.int32, (256, 256), 0)
            pick = jnp.where(slot == targets_ref[s : s + 1, :], 1.0, 0.0).astype(BF16)
            wide_ref[...] = rows_ref[s].reshape(2048, 128).astype(F32)
            for q in range(8):
                part = wide_ref[pl.ds(q, 256, stride=8), :].astype(BF16)
                chosen_ref[256 * s : 256 * s + 256, 128 * q : 128 * q + 128] = dot(pick, part, (0, 0)).astype(BF16)
        dots = dot(chosen_ref[...], chosen_ref[...], (1, 1))
        row = lax.broadcasted_iota(jnp.int32, (512, 512), 0)
        col = lax.broadcasted_iota(jnp.int32, (512, 512), 1)
        own = jnp.where(row == col, dots, 0.0)
        norm_row = jnp.sum(own, axis=0, keepdims=True)
        norm_ref[...] = norm_row
        w_ref[...] = dots / (jnp.sum(own, axis=1, keepdims=True) + norm_row - dots)
        cholesky_inverse(w_ref, diag_ref)
        inv_ref[...] = lower_blocks(w_ref[...])
        gram_ref[...] = jnp.zeros_like(gram_ref)

    emb = emb_ref[...]
    wide = emb.astype(F32)
    norms = jnp.sum(wide * wide, axis=1, keepdims=True)
    dots = dot(emb, chosen_ref[...], (1, 1))
    similar = dots / (norms + norm_ref[...] - dots)
    factor = dot(similar, inv_ref[...], (1, 1), HI)
    factor_ref[...] = factor
    for b, (i, j) in enumerate(UPPER):
        if i == j:
            part = dot(factor[:, 128 * i : 128 * i + 128], factor[:, 128 * i :], (0, 0), HI)
            for e in range(4 - i):
                gram_ref[b + e] += part[:, 128 * e : 128 * e + 128]


def factor_call(targets, rows, embeddings):
    count = embeddings.shape[0] // TILE
    vmem = lambda shape: pl.BlockSpec(shape, lambda i: (0,) * len(shape))
    return pl.pallas_call(
        factor_kernel,
        grid=(count,),
        out_shape=(
            jax.ShapeDtypeStruct((embeddings.shape[0], 512), F32),
            jax.ShapeDtypeStruct((10, 128, 128), F32),
        ),
        in_specs=[vmem((2, 256)), vmem((2, 256, 8, 128)), pl.BlockSpec((TILE, 1024), lambda i: (i, 0))],
        out_specs=(pl.BlockSpec((TILE, 512), lambda i: (i, 0)), vmem((10, 128, 128))),
        scratch_shapes=[
            pltpu.VMEM((2048, 128), F32),
            pltpu.VMEM((512, 1024), BF16),
            pltpu.VMEM((512, 512), F32),
            pltpu.VMEM((512, 512), F32),
            pltpu.VMEM((8, NB, 128), F32),
            pltpu.VMEM((1, 512), F32),
        ],
        compiler_params=pltpu.CompilerParams(vmem_limit_bytes=56 << 20, dimension_semantics=("arbitrary",)),
        name="factor",
    )(targets, rows, embeddings)


STREAMS = ((0, 384), (384, 256))


def reduce_kernel(in_ref, out_ref, core_in, big_in, small_in, z_in, half_sum, big_sum, small_sum, send, recv):
    x, y, z, core = coords()
    other = (lax.axis_index("bank"), 1 - core)
    along_x, along_y, along_z = axis_peers(x, y, z, core)
    greet([other] + along_x + along_y + along_z)
    count = [0]
    everything = []

    def push(src, dst, peer):
        i = count[0]
        count[0] += 1
        copy = pltpu.make_async_remote_copy(
            src_ref=src, dst_ref=dst, send_sem=send.at[i], recv_sem=recv.at[i], device_id=peer, device_id_type=MESH
        )
        copy.start()
        everything.append(copy)
        return copy

    mine = core * 640
    theirs = (1 - core) * 640
    axes = ((along_x, NX, x), (along_y, NY, y))
    state = []
    for s, (start, size) in enumerate(STREAMS):
        state.append(push(in_ref.at[pl.ds(theirs + start, size)], core_in.at[pl.ds(start, size)], other))
    big = []
    for s, (start, size) in enumerate(STREAMS):
        peers, n, pos = axes[s]
        state[s].wait_recv()
        half_sum[pl.ds(start, size), :] = in_ref[pl.ds(mine + start, size), :] + core_in[pl.ds(start, size), :]
        part = size // 4
        copies = []
        for o in range(1, n):
            to = lax.rem(pos + o, n)
            copies.append(
                push(
                    half_sum.at[pl.ds(start + to * part, part)],
                    big_in.at[o - 1, pl.ds(start // 4, part)],
                    peers[o - 1],
                )
            )
        big.append(copies)
    small = []
    for s, (start, size) in enumerate(STREAMS):
        _, n, pos = axes[s]
        peers, n2, pos2 = axes[1 - s]
        part = size // 4
        for copy in big[s]:
            copy.wait_recv()
        total = half_sum[pl.ds(start + pos * part, part), :]
        for o in range(n - 1):
            total = total + big_in[o, start // 4 : start // 4 + part, :]
        big_sum[start // 4 : start // 4 + part, :] = total
        tiny = part // 4
        copies = []
        for o in range(1, n2):
            to = lax.rem(pos2 + o, n2)
            copies.append(
                push(
                    big_sum.at[pl.ds(start // 4 + to * tiny, tiny)],
                    small_in.at[o - 1, pl.ds(start // 16, tiny)],
                    peers[o - 1],
                )
            )
        small.append(copies)
    last = []
    for s, (start, size) in enumerate(STREAMS):
        _, n2, pos2 = axes[1 - s]
        tiny = size // 16
        for copy in small[s]:
            copy.wait_recv()
        total = big_sum[pl.ds(start // 4 + pos2 * tiny, tiny), :]
        for o in range(n2 - 1):
            total = total + small_in[o, start // 16 : start // 16 + tiny, :]
        small_sum[start // 16 : start // 16 + tiny, :] = total
        piece = small_sum.at[pl.ds(start // 16, tiny)]
        last.append([push(piece, z_in.at[z, pl.ds(start // 16, tiny)], peer) for peer in along_z])
        z_in[z, start // 16 : start // 16 + tiny, :] = total
    back = []
    for s, (start, size) in enumerate(STREAMS):
        _, n, pos = axes[s]
        peers, n2, pos2 = axes[1 - s]
        part, tiny = size // 4, size // 16
        for copy in last[s]:
            copy.wait_recv()
        total = z_in[0, start // 16 : start // 16 + tiny, :]
        for o in range(1, NZ):
            total = total + z_in[o, start // 16 : start // 16 + tiny, :]
        at = mine + start + pos * part + pos2 * tiny
        out_ref[pl.ds(at, tiny), :] = total
        piece = out_ref.at[pl.ds(at, tiny)]
        back.append([push(piece, piece, peer) for peer in peers])
    far = []
    for s, (start, size) in enumerate(STREAMS):
        peers, n, pos = axes[s]
        part = size // 4
        for copy in back[s]:
            copy.wait_recv()
        piece = out_ref.at[pl.ds(mine + start + pos * part, part)]
        far.append([push(piece, piece, peer) for peer in peers])
    final = []
    for s, (start, size) in enumerate(STREAMS):
        for copy in far[s]:
            copy.wait_recv()
        piece = out_ref.at[pl.ds(mine + start, size)]
        final.append(push(piece, piece, other))
    for copy in final:
        copy.wait_recv()
    for copy in everything:
        copy.wait_send()


def reduce_gram(gram):
    copies = 2 * (1 + 3 + 3 + 7 + 3 + 3 + 1)
    return pl.pallas_call(
        reduce_kernel,
        out_shape=jax.ShapeDtypeStruct((1280, 128), F32),
        in_specs=[pl.BlockSpec(memory_space=pltpu.VMEM)],
        out_specs=pl.BlockSpec(memory_space=pltpu.VMEM),
        scratch_shapes=[
            pltpu.VMEM((640, 128), F32),
            pltpu.VMEM((3, 160, 128), F32),
            pltpu.VMEM((3, 40, 128), F32),
            pltpu.VMEM((NZ, 40, 128), F32),
            pltpu.VMEM((640, 128), F32),
            pltpu.VMEM((160, 128), F32),
            pltpu.VMEM((40, 128), F32),
            pltpu.SemaphoreType.DMA((copies,)),
            pltpu.SemaphoreType.DMA((copies,)),
        ],
        compiler_params=pltpu.CompilerParams(collective_id=1, has_side_effects=True),
        name="reduce_gram",
    )(gram.reshape(1280, 128)).reshape(10, 128, 128)


def basis_kernel(total_rows, gram_ref, factor_ref, basis_ref, triangle_ref, w_ref, inv_ref, diag_ref):
    @pl.when(pl.program_id(0) == 0)
    def _():
        for b, (i, j) in enumerate(UPPER):
            w_ref[128 * i : 128 * i + 128, 128 * j : 128 * j + 128] = gram_ref[b] / total_rows
        cholesky_inverse(w_ref, diag_ref)
        w = w_ref[...]
        inv_ref[...] = lower_blocks(w)
        row = lax.broadcasted_iota(jnp.int32, (512, 512), 0)
        col = lax.broadcasted_iota(jnp.int32, (512, 512), 1)
        triangle_ref[...] = jnp.where(row < col, w, 0.0)
        low = lax.broadcasted_iota(jnp.int32, (NB, 128), 1)
        sub = lax.broadcasted_iota(jnp.int32, (NB, 128), 0)
        for k in range(8):
            left = 128 * (k // 2)
            both = diag_ref[k]
            keep = triangle_ref[NB * k : NB * k + NB, left : left + 128]
            if k % 2:
                mine = pltpu.roll(both, 64, 1)
                keep = jnp.where(low >= 64, jnp.where(low - 64 >= sub, mine, 0.0), keep)
            else:
                keep = jnp.where(low < 64, jnp.where(low >= sub, both, 0.0), keep)
            triangle_ref[NB * k : NB * k + NB, left : left + 128] = keep

    factor = factor_ref[...]
    inverse = inv_ref[...]
    basis_ref[:, :256] = dot(factor[:, :256], inverse[:256, :256], (1, 1), HI)
    basis_ref[:, 256:] = dot(factor, inverse[256:, :], (1, 1), HI)


def basis_call(gram, factor, total_rows):
    import functools

    count = factor.shape[0] // TILE
    vmem = lambda shape: pl.BlockSpec(shape, lambda i: (0,) * len(shape))
    return pl.pallas_call(
        functools.partial(basis_kernel, total_rows),
        grid=(count,),
        out_shape=(jax.ShapeDtypeStruct(factor.shape, F32), jax.ShapeDtypeStruct((512, 512), F32)),
        in_specs=[vmem((10, 128, 128)), pl.BlockSpec((TILE, 512), lambda i: (i, 0))],
        out_specs=(pl.BlockSpec((TILE, 512), lambda i: (i, 0)), vmem((512, 512))),
        scratch_shapes=[pltpu.VMEM((512, 512), F32), pltpu.VMEM((512, 512), F32), pltpu.VMEM((8, NB, 128), F32)],
        compiler_params=pltpu.CompilerParams(vmem_limit_bytes=56 << 20, dimension_semantics=("arbitrary",)),
        name="basis",
    )(gram, factor)


def per_device(embeddings, pivots):
    row_count = embeddings.shape[0]
    device_count = lax.axis_size(("bank", "sub"))
    me = lax.axis_index(("bank", "sub"))
    owner = pivots // row_count
    local = jnp.sum(jnp.where(owner == me, pivots - me * row_count, 0), axis=1)
    mine = jnp.stack([lax.dynamic_slice(embeddings, (local[s], 0), (1, 1024)).reshape(8, 128) for s in range(2)])
    bank, core = owner // 2, owner % 2
    bx, bz, by = bank % NX, (bank // NX) % NZ, bank // (NX * NZ)
    targets = jnp.stack([(core * 128 + bank)[0], (core * 128 + (bx * NZ + bz) * NY + by)[1]])
    rows = gather_rows(mine)
    factor, gram = factor_call(targets, rows, embeddings)
    gram = reduce_gram(gram)
    return basis_call(gram, factor, float(row_count * device_count))


def solution(mesh):
    in_specs = (P(("bank", "sub"), None), P())
    out_specs = (P(("bank", "sub"), None), P())
    return jax.shard_map(per_device, mesh=mesh, in_specs=in_specs, out_specs=out_specs, check_vma=False)
```

time: 716 us -> 149 us (0.21)
  waiting for transfers between devices: 252 us -> 0 us
  other arithmetic: 243 us -> 2.07 us
  Pallas kernels: 0 us -> 140 us
  blocking collectives: 90.1 us -> 0 us
  matrix products: 67.7 us -> 0 us
  local copies, waits for them, and re-layouts: 37.6 us -> 1.36 us
  between operations: 19.8 us -> 4.57 us
    psum x1 -> x0, waiting for transfers between devices: 252 us -> none  [per_device(): gram = lax.psum(local_gram, ('bank', 'sub'))]
    another operation x35 -> x2, other arithmetic: 230 us -> 1.19 us  [the longest x1 0.6 us: per_device(): jnp.stack([lax.dynamic_slice(embeddings, (local[s], 0), (1, 1024)).reshap...]
    pallas_call x0 -> x4, Pallas kernels: none -> 140 us  [the longest x1 50.4 us: factor_call(): pl.pallas_call(factor_kernel, grid=(count,), out_shape=(jax.ShapeDtypeStr...]
    psum x1 -> x0, blocking collectives: 90.1 us -> none  [per_device(): chosen = lax.psum(picked, ('bank', 'sub')).astype(jnp.bfloat16)]
    dot_general x9 -> x0, matrix products: 50.2 us -> none  [the longest x6 31.8 us: times_transposed(): lax.dot_general(left, right, (((1,), (1,)), ((), ())), precision=lax.Prec...]
    another operation x36 -> x0, local copies, waits for them, and re-layouts: 22.6 us -> none
    another operation x23 -> x0, matrix products: 17.5 us -> none  [the longest x13 8.74 us: lower_inverse(): lax.linalg.triangular_solve(factor, identity, left_side=True, lower=True)]
  transfers between devices with their start and end apart: 1 -> 0, of which waited for: 1 -> 0; matrix products, arithmetic and copies ran while one was open for 0% -> 0% of each run, Pallas kernels for 0% -> 0%
where the time goes in v1:
time: 149 us; the launch traced here: 148 us
  Pallas kernels  140 us (94%)
  between operations  4.57 us (3%)
  other arithmetic  2.07 us (1%)
    pallas_call x1, Pallas kernels, factor_call(): pl.pallas_call(factor_kernel, grid=(count,), out_shape=(jax.ShapeDtypeStr...  50.4 us
    pallas_call x1, Pallas kernels, basis_call(): pl.pallas_call(functools.partial(basis_kernel, total_rows), grid=(count,)...  32.5 us
    pallas_call x1, Pallas kernels, reduce_gram(): pl.pallas_call(reduce_kernel, out_shape=jax.ShapeDtypeStruct((1280, 128),...  30.3 us
    pallas_call x1, Pallas kernels, gather_rows(): pl.pallas_call(gather_kernel, out_shape=jax.ShapeDtypeStruct((2, 256, 8,...  27.3 us

profile of v1, /device:TPU:1, one launch (start us, length us, event | category | flops | bytes accessed | tf_op | source)
XLA Modules:
  0.0 148.5 jit_solution(16510709486601868208)
XLA Ops:
  0.6 0.8 fusion.3
  1.4 0.6 fusion.8
  5.9 0.8 dynamic-slice_reduce_fusion.1
  6.7 0.6 pad_maximum_fusion.mine_ref
  7.4 0.6 pad_add_fusion.targets_ref
  8.0 27.3 %gather_rows.1.rows_ref = bf16[2,256,8,128]{3,2,1,0:T(8,128)(2,1)} custom-call(bf16[2,8,128]{2,1,0:T(8,128)(2,1)} %pad_maximum_fusion.mine_ref), custom_call_target="tpu_custom_call" | custom-call | tf_op jit(solution)/shard_map/gather_rows/pallas_call | solution.py:171
  35.3 50.4 %factor.1 = (f32[3072,512]{1,0:T(8,128)}, f32[10,128,128]{2,1,0:T(8,128)}) custom-call(s32[2,256]{1,0:T(2,128)} %pad_add_fusion.targets_ref, bf16[2,256,8,128]{3,2,1,0:T(8,128)(2,1)} %gather_rows.1.rows_ref, bf16[3072,1024]{1,0:T(8,128)(2,1)} %emb_ref.1), custom_call_target="tpu_custom_call" | custom-call | tf_op jit(solution)/shard_map/factor/pallas_call | solution.py:222
  85.7 30.3 %reduce_gram.1 = f32[1280,128]{1,0:T(8,128)} custom-call(f32[1280,128]{1,0:T(8,128)} %bitcast.7), custom_call_target="tpu_custom_call" | custom-call | tf_op jit(solution)/shard_map/reduce_gram/pallas_call | solution.py:360
  116.0 32.5 %basis.1 = (f32[3072,512]{1,0:T(8,128)}, f32[512,512]{1,0:T(8,128)}) custom-call(f32[10,128,128]{2,1,0:T(8,128)} %bitcast.6, f32[3072,512]{1,0:T(8,128)} %get-tuple-element.5.factor_ref), custom_call_target="tpu_custom_call" | custom-call | tf_op jit(solution)/shard_map/basis/pallas_call | solution.py:416
  (5 shorter events, 0.1 us)

commit v2 on v1

--- a/solution.py
+++ b/solution.py
@@ -1,3 +1,5 @@
+import functools
+
 import jax
 import jax.numpy as jnp
 from jax import lax
@@ -46,7 +48,7 @@
     return out
 
 
-def cholesky_inverse(w_ref, diag_ref):
+def cholesky_steps(w_ref, diag_ref):
     n = w_ref.shape[0]
     lane = lax.broadcasted_iota(jnp.int32, (8, 128), 1)
     sub = lax.broadcasted_iota(jnp.int32, (8, 128), 0)
@@ -61,6 +63,7 @@
             rows.append(jnp.where(lane < 64, block, jnp.where(lane - 64 == sub + 8 * t, 1.0, 0.0)))
         both = jnp.concatenate(base_block(rows), axis=0)
         diag_ref[k] = both
+        yield
         wide = w_ref[r0 : r0 + NB, :]
         col = lax.broadcasted_iota(jnp.int32, (NB, n), 1)
         row = lax.broadcasted_iota(jnp.int32, (NB, n), 0)
@@ -74,6 +77,12 @@
             col = lax.broadcasted_iota(jnp.int32, (rest, n), 1)
             current = jnp.where((col >= r0) & (col < r0 + NB), 0.0, current)
             w_ref[r0 + NB :, :] = current - update
+        yield
+
+
+def cholesky_inverse(w_ref, diag_ref):
+    for _ in cholesky_steps(w_ref, diag_ref):
+        pass
 
 
 def lower_blocks(w):
@@ -179,7 +188,15 @@
     )(mine)
 
 
-def factor_kernel(targets_ref, rows_ref, emb_ref, factor_ref, gram_ref, wide_ref, chosen_ref, w_ref, inv_ref, diag_ref, norm_ref):
+LEAD = 16
+
+
+def split(v):
+    high = v.astype(BF16)
+    return high, (v - high.astype(F32)).astype(BF16)
+
+
+def similar_kernel(targets_ref, rows_ref, emb_ref, high_ref, low_ref, gram_ref, block_ref, r_ref, wide_ref, chosen_ref, norm_ref, own_ref):
     step = pl.program_id(0)
 
     @pl.when(step == 0)
@@ -197,54 +214,78 @@
         own = jnp.where(row == col, dots, 0.0)
         norm_row = jnp.sum(own, axis=0, keepdims=True)
         norm_ref[...] = norm_row
-        w_ref[...] = dots / (jnp.sum(own, axis=1, keepdims=True) + norm_row - dots)
-        cholesky_inverse(w_ref, diag_ref)
-        inv_ref[...] = lower_blocks(w_ref[...])
+        block = dots / (jnp.sum(own, axis=1, keepdims=True) + norm_row - dots)
+        block_ref[...] = block
+        lead = jnp.sum(jnp.where(col < LEAD, block, 0.0), axis=1, keepdims=True) * (1.0 / LEAD)
+        use = (row >= LEAD) & (row != col)
+        above = jnp.sum(jnp.where(use, block * lead, 0.0), axis=0, keepdims=True)
+        below = jnp.sum(jnp.where(use, lead * lead, 0.0), axis=0, keepdims=True)
+        ratio = above / jnp.where(below > 0.0, below, 1.0)
+        ratio = jnp.where(below > 0.0, jnp.clip(ratio, -4.0, 4.0), 0.0)
+        r_ref[...] = jnp.where(lax.broadcasted_iota(jnp.int32, (1, 512), 1) < LEAD, 0.0, ratio)
         gram_ref[...] = jnp.zeros_like(gram_ref)
+        own_ref[...] = jnp.zeros_like(own_ref)
 
     emb = emb_ref[...]
     wide = emb.astype(F32)
     norms = jnp.sum(wide * wide, axis=1, keepdims=True)
     dots = dot(emb, chosen_ref[...], (1, 1))
     similar = dots / (norms + norm_ref[...] - dots)
-    factor = dot(similar, inv_ref[...], (1, 1), HI)
-    factor_ref[...] = factor
+    lane = lax.broadcasted_iota(jnp.int32, (TILE, 128), 1)
+    lead = jnp.sum(jnp.where(lane < LEAD, similar[:, :128], 0.0), axis=1, keepdims=True) * (1.0 / LEAD)
+    similar = similar - lead * r_ref[...]
+    high, low = split(similar)
+    high_ref[...] = high
+    low_ref[...] = low
+    own_ref[...] += jnp.sum(low.astype(F32) * low.astype(F32), axis=0, keepdims=True)
     for b, (i, j) in enumerate(UPPER):
         if i == j:
-            part = dot(factor[:, 128 * i : 128 * i + 128], factor[:, 128 * i :], (0, 0), HI)
+            left_high, left_low = high[:, 128 * i : 128 * i + 128], low[:, 128 * i : 128 * i + 128]
+            part = dot(left_high, high[:, 128 * i :], (0, 0))
+            part += dot(left_high, low[:, 128 * i :], (0, 0)) + dot(left_low, high[:, 128 * i :], (0, 0))
             for e in range(4 - i):
                 gram_ref[b + e] += part[:, 128 * e : 128 * e + 128]
 
-
-def factor_call(targets, rows, embeddings):
+    @pl.when(step == pl.num_programs(0) - 1)
+    def _():
+        row = lax.broadcasted_iota(jnp.int32, (128, 128), 0)
+        col = lax.broadcasted_iota(jnp.int32, (128, 128), 1)
+        for b, (i, j) in enumerate(UPPER):
+            if i == j:
+                gram_ref[b] += jnp.where(row == col, own_ref[:, 128 * i : 128 * i + 128], 0.0)
+
+
+def similar_call(targets, rows, embeddings):
     count = embeddings.shape[0] // TILE
-    vmem = lambda shape: pl.BlockSpec(shape, lambda i: (0,) * len(shape))
+    whole = lambda shape: pl.BlockSpec(shape, lambda i: (0,) * len(shape))
+    tile = lambda width: pl.BlockSpec((TILE, width), lambda i: (i, 0))
     return pl.pallas_call(
-        factor_kernel,
+        similar_kernel,
         grid=(count,),
         out_shape=(
-            jax.ShapeDtypeStruct((embeddings.shape[0], 512), F32),
+            jax.ShapeDtypeStruct((embeddings.shape[0], 512), BF16),
+            jax.ShapeDtypeStruct((embeddings.shape[0], 512), BF16),
             jax.ShapeDtypeStruct((10, 128, 128), F32),
+            jax.ShapeDtypeStruct((512, 512), F32),
+            jax.ShapeDtypeStruct((1, 512), F32),
         ),
-        in_specs=[vmem((2, 256)), vmem((2, 256, 8, 128)), pl.BlockSpec((TILE, 1024), lambda i: (i, 0))],
-        out_specs=(pl.BlockSpec((TILE, 512), lambda i: (i, 0)), vmem((10, 128, 128))),
+        in_specs=[whole((2, 256)), whole((2, 256, 8, 128)), tile(1024)],
+        out_specs=(tile(512), tile(512), whole((10, 128, 128)), whole((512, 512)), whole((1, 512))),
         scratch_shapes=[
             pltpu.VMEM((2048, 128), F32),
             pltpu.VMEM((512, 1024), BF16),
-            pltpu.VMEM((512, 512), F32),
-            pltpu.VMEM((512, 512), F32),
-            pltpu.VMEM((8, NB, 128), F32),
+            pltpu.VMEM((1, 512), F32),
             pltpu.VMEM((1, 512), F32),
         ],
         compiler_params=pltpu.CompilerParams(vmem_limit_bytes=56 << 20, dimension_semantics=("arbitrary",)),
-        name="factor",
+        name="similar",
     )(targets, rows, embeddings)
 
 
 STREAMS = ((0, 384), (384, 256))
 
 
-def reduce_kernel(in_ref, out_ref, core_in, big_in, small_in, z_in, half_sum, big_sum, small_sum, send, recv):
+def reduce_kernel(in_ref, block_ref, r_ref, out_ref, tail_ref, w_ref, diag_ref, core_in, big_in, small_in, z_in, half_sum, big_sum, small_sum, send, recv):
     x, y, z, core = coords()
     other = (lax.axis_index("bank"), 1 - core)
     along_x, along_y, along_z = axis_peers(x, y, z, core)
@@ -262,6 +303,8 @@
         everything.append(copy)
         return copy
 
+    w_ref[...] = block_ref[...]
+    work = cholesky_steps(w_ref, diag_ref)
     mine = core * 640
     theirs = (1 - core) * 640
     axes = ((along_x, NX, x), (along_y, NY, y))
@@ -271,6 +314,7 @@
     big = []
     for s, (start, size) in enumerate(STREAMS):
         peers, n, pos = axes[s]
+        next(work)
         state[s].wait_recv()
         half_sum[pl.ds(start, size), :] = in_ref[pl.ds(mine + start, size), :] + core_in[pl.ds(start, size), :]
         part = size // 4
@@ -290,6 +334,7 @@
         _, n, pos = axes[s]
         peers, n2, pos2 = axes[1 - s]
         part = size // 4
+        next(work)
         for copy in big[s]:
             copy.wait_recv()
         total = half_sum[pl.ds(start + pos * part, part), :]
@@ -312,6 +357,7 @@
     for s, (start, size) in enumerate(STREAMS):
         _, n2, pos2 = axes[1 - s]
         tiny = size // 16
+        next(work)
         for copy in small[s]:
             copy.wait_recv()
         total = big_sum[pl.ds(start // 4 + pos2 * tiny, tiny), :]
@@ -326,6 +372,7 @@
         _, n, pos = axes[s]
         peers, n2, pos2 = axes[1 - s]
         part, tiny = size // 4, size // 16
+        next(work)
         for copy in last[s]:
             copy.wait_recv()
         total = z_in[0, start // 16 : start // 16 + tiny, :]
@@ -339,30 +386,39 @@
     for s, (start, size) in enumerate(STREAMS):
         peers, n, pos = axes[s]
         part = size // 4
+        next(work)
         for copy in back[s]:
             copy.wait_recv()
         piece = out_ref.at[pl.ds(mine + start + pos * part, part)]
         far.append([push(piece, piece, peer) for peer in peers])
     final = []
     for s, (start, size) in enumerate(STREAMS):
+        next(work)
         for copy in far[s]:
             copy.wait_recv()
         piece = out_ref.at[pl.ds(mine + start, size)]
         final.append(push(piece, piece, other))
+    for _ in work:
+        pass
+    inverse = lower_blocks(w_ref[...])
+    weight = jnp.sum(inverse * r_ref[...], axis=1, keepdims=True) * (1.0 / LEAD)
+    tail_ref[...] = inverse + jnp.where(lax.broadcasted_iota(jnp.int32, (512, 512), 1) < LEAD, weight, 0.0)
     for copy in final:
         copy.wait_recv()
     for copy in everything:
         copy.wait_send()
 
 
-def reduce_gram(gram):
+def reduce_gram(gram, block, ratio):
     copies = 2 * (1 + 3 + 3 + 7 + 3 + 3 + 1)
-    return pl.pallas_call(
+    total, tail = pl.pallas_call(
         reduce_kernel,
-        out_shape=jax.ShapeDtypeStruct((1280, 128), F32),
-        in_specs=[pl.BlockSpec(memory_space=pltpu.VMEM)],
-        out_specs=pl.BlockSpec(memory_space=pltpu.VMEM),
+        out_shape=(jax.ShapeDtypeStruct((1280, 128), F32), jax.ShapeDtypeStruct((512, 512), F32)),
+        in_specs=[pl.BlockSpec(memory_space=pltpu.VMEM)] * 3,
+        out_specs=(pl.BlockSpec(memory_space=pltpu.VMEM),) * 2,
         scratch_shapes=[
+            pltpu.VMEM((512, 512), F32),
+            pltpu.VMEM((8, NB, 128), F32),
             pltpu.VMEM((640, 128), F32),
             pltpu.VMEM((3, 160, 128), F32),
             pltpu.VMEM((3, 40, 128), F32),
@@ -373,72 +429,109 @@
             pltpu.SemaphoreType.DMA((copies,)),
             pltpu.SemaphoreType.DMA((copies,)),
         ],
-        compiler_params=pltpu.CompilerParams(collective_id=1, has_side_effects=True),
+        compiler_params=pltpu.CompilerParams(collective_id=1, has_side_effects=True, vmem_limit_bytes=48 << 20),
         name="reduce_gram",
-    )(gram.reshape(1280, 128)).reshape(10, 128, 128)
-
-
-def basis_kernel(total_rows, gram_ref, factor_ref, basis_ref, triangle_ref, w_ref, inv_ref, diag_ref):
+    )(gram.reshape(1280, 128), block, ratio)
+    return total.reshape(10, 128, 128), tail
+
+
+def basis_kernel(total_rows, gram_ref, tail_ref, high_ref, low_ref, basis_ref, triangle_ref, w_ref, diag_ref, inv_high, inv_low):
     @pl.when(pl.program_id(0) == 0)
     def _():
         for b, (i, j) in enumerate(UPPER):
             w_ref[128 * i : 128 * i + 128, 128 * j : 128 * j + 128] = gram_ref[b] / total_rows
         cholesky_inverse(w_ref, diag_ref)
         w = w_ref[...]
-        inv_ref[...] = lower_blocks(w)
+        inv_high[...], inv_low[...] = split(lower_blocks(w))
         row = lax.broadcasted_iota(jnp.int32, (512, 512), 0)
         col = lax.broadcasted_iota(jnp.int32, (512, 512), 1)
-        triangle_ref[...] = jnp.where(row < col, w, 0.0)
-        low = lax.broadcasted_iota(jnp.int32, (NB, 128), 1)
+        w_ref[...] = jnp.where(row < col, w, 0.0)
+        lane = lax.broadcasted_iota(jnp.int32, (NB, 128), 1)
         sub = lax.broadcasted_iota(jnp.int32, (NB, 128), 0)
         for k in range(8):
             left = 128 * (k // 2)
             both = diag_ref[k]
-            keep = triangle_ref[NB * k : NB * k + NB, left : left + 128]
+            keep = w_ref[NB * k : NB * k + NB, left : left + 128]
             if k % 2:
                 mine = pltpu.roll(both, 64, 1)
-                keep = jnp.where(low >= 64, jnp.where(low - 64 >= sub, mine, 0.0), keep)
+                keep = jnp.where(lane >= 64, jnp.where(lane - 64 >= sub, mine, 0.0), keep)
             else:
-                keep = jnp.where(low < 64, jnp.where(low >= sub, both, 0.0), keep)
-            triangle_ref[NB * k : NB * k + NB, left : left + 128] = keep
-
-    factor = factor_ref[...]
-    inverse = inv_ref[...]
-    basis_ref[:, :256] = dot(factor[:, :256], inverse[:256, :256], (1, 1), HI)
-    basis_ref[:, 256:] = dot(factor, inverse[256:, :], (1, 1), HI)
-
-
-def basis_call(gram, factor, total_rows):
-    import functools
-
-    count = factor.shape[0] // TILE
-    vmem = lambda shape: pl.BlockSpec(shape, lambda i: (0,) * len(shape))
+                keep = jnp.where(lane < 64, jnp.where(lane >= sub, both, 0.0), keep)
+            w_ref[NB * k : NB * k + NB, left : left + 128] = keep
+        triangle_ref[...] = dot(w_ref[...], tail_ref[...], (1, 1), HI)
+
+    high, low = high_ref[...], low_ref[...]
+    for start, depth in ((0, 256), (256, 512)):
+        right_high, right_low = inv_high[start : start + 256, :depth], inv_low[start : start + 256, :depth]
+        out = dot(low[:, :depth], right_high, (1, 1)) + dot(high[:, :depth], right_low, (1, 1))
+        basis_ref[:, start : start + 256] = out + dot(high[:, :depth], right_high, (1, 1))
+
+
+def basis_call(gram, tail, high, low, total_rows):
+    count = high.shape[0] // TILE
+    whole = lambda shape: pl.BlockSpec(shape, lambda i: (0,) * len(shape))
+    tile = pl.BlockSpec((TILE, 512), lambda i: (i, 0))
     return pl.pallas_call(
         functools.partial(basis_kernel, total_rows),
         grid=(count,),
-        out_shape=(jax.ShapeDtypeStruct(factor.shape, F32), jax.ShapeDtypeStruct((512, 512), F32)),
-        in_specs=[vmem((10, 128, 128)), pl.BlockSpec((TILE, 512), lambda i: (i, 0))],
-        out_specs=(pl.BlockSpec((TILE, 512), lambda i: (i, 0)), vmem((512, 512))),
-        scratch_shapes=[pltpu.VMEM((512, 512), F32), pltpu.VMEM((512, 512), F32), pltpu.VMEM((8, NB, 128), F32)],
+        out_shape=(jax.ShapeDtypeStruct(high.shape, F32), jax.ShapeDtypeStruct((512, 512), F32)),
+        in_specs=[whole((10, 128, 128)), whole((512, 512)), tile, tile],
+        out_specs=(tile, whole((512, 512))),
+        scratch_shapes=[
+            pltpu.VMEM((512, 512), F32),
+            pltpu.VMEM((8, NB, 128), F32),
+            pltpu.VMEM((512, 512), BF16),
+            pltpu.VMEM((512, 512), BF16),
+        ],
         compiler_params=pltpu.CompilerParams(vmem_limit_bytes=56 << 20, dimension_semantics=("arbitrary",)),
         name="basis",
-    )(gram, factor)
+    )(gram, tail, high, low)
+
+
+def pick_kernel(row_count, pivots_ref, emb_ref, mine_ref, targets_ref, block_ref, sems):
+    start = (lax.axis_index("bank") * 2 + lax.axis_index("sub")) * row_count
+    pivots = pivots_ref[...]
+    inside = (pivots >= start) & (pivots < start + row_count)
+    copies, offsets = [], []
+    for s in range(2):
+        local = jnp.sum(jnp.where(inside[s : s + 1], pivots[s : s + 1] - start, 0))
+        first = pl.multiple_of((local // 16) * 16, 16)
+        copy = pltpu.make_async_copy(emb_ref.at[pl.ds(first, 16)], block_ref.at[s], sems.at[s])
+        copy.start()
+        copies.append(copy)
+        offsets.append(local - first)
+    owner = jnp.floor((pivots.astype(F32) + 0.5) * (1.0 / row_count)).astype(jnp.int32)
+    bank, core = owner >> 1, owner & 1
+    bx, bz, by = bank & (NX - 1), (bank >> 2) & (NZ - 1), bank >> 5
+    first = core * 128 + bank
+    second = core * 128 + (bx * NZ + bz) * NY + by
+    targets_ref[...] = jnp.where(lax.broadcasted_iota(jnp.int32, (2, 256), 0) == 0, first, second)
+    for s in range(2):
+        copies[s].wait()
+        rows = block_ref[s].astype(F32)
+        keep = lax.broadcasted_iota(jnp.int32, (16, 1024), 0) == offsets[s]
+        row = jnp.sum(jnp.where(keep, rows, 0.0), axis=0, keepdims=True)
+        mine_ref[s] = jnp.concatenate([row[:, 128 * q : 128 * q + 128] for q in range(8)], axis=0).astype(BF16)
+
+
+def pick_rows(pivots, embeddings):
+    return pl.pallas_call(
+        functools.partial(pick_kernel, embeddings.shape[0]),
+        out_shape=(jax.ShapeDtypeStruct((2, 8, 128), BF16), jax.ShapeDtypeStruct((2, 256), jnp.int32)),
+        in_specs=[pl.BlockSpec(memory_space=pltpu.VMEM), pl.BlockSpec(memory_space=pl.ANY)],
+        out_specs=(pl.BlockSpec(memory_space=pltpu.VMEM),) * 2,
+        scratch_shapes=[pltpu.VMEM((2, 16, 1024), BF16), pltpu.SemaphoreType.DMA((2,))],
+        name="pick_rows",
+    )(pivots, embeddings)
 
 
 def per_device(embeddings, pivots):
-    row_count = embeddings.shape[0]
-    device_count = lax.axis_size(("bank", "sub"))
-    me = lax.axis_index(("bank", "sub"))
-    owner = pivots // row_count
-    local = jnp.sum(jnp.where(owner == me, pivots - me * row_count, 0), axis=1)
-    mine = jnp.stack([lax.dynamic_slice(embeddings, (local[s], 0), (1, 1024)).reshape(8, 128) for s in range(2)])
-    bank, core = owner // 2, owner % 2
-    bx, bz, by = bank % NX, (bank // NX) % NZ, bank // (NX * NZ)
-    targets = jnp.stack([(core * 128 + bank)[0], (core * 128 + (bx * NZ + bz) * NY + by)[1]])
+    total_rows = embeddings.shape[0] * lax.axis_size(("bank", "sub"))
+    mine, targets = pick_rows(pivots, embeddings)
     rows = gather_rows(mine)
-    factor, gram = factor_call(targets, rows, embeddings)
-    gram = reduce_gram(gram)
-    return basis_call(gram, factor, float(row_count * device_count))
+    high, low, gram, block, ratio = similar_call(targets, rows, embeddings)
+    gram, tail = reduce_gram(gram, block, ratio)
+    return basis_call(gram, tail, high, low, float(total_rows))
 
 
 def solution(mesh):

time: 149 us -> 124 us (0.83)
  Pallas kernels: 140 us -> 118 us
  between operations: 4.57 us -> 0.68 us
  local copies, waits for them, and re-layouts: 1.36 us -> 4.79 us
  other arithmetic: 2.07 us -> 0 us
    pallas_call x2 -> x3, Pallas kernels: 80.7 us -> 58.3 us  [the longest x1 39.9 us: reduce_gram(): pl.pallas_call(reduce_kernel, out_shape=(jax.ShapeDtypeStruct((1280, 128)...]
    unnamed x0 -> x10, local copies, waits for them, and re-layouts: none -> 4.79 us
where the time goes in v2:
time: 124 us; the launch traced here: 123 us
  Pallas kernels  118 us (95%)
  local copies, waits for them, and re-layouts  4.79 us (4%)
    pallas_call x1, Pallas kernels, reduce_gram(): pl.pallas_call(reduce_kernel, out_shape=(jax.ShapeDtypeStruct((1280, 128)...  39.9 us
    pallas_call x1, Pallas kernels, basis_call(): pl.pallas_call(functools.partial(basis_kernel, total_rows), grid=(count,)...  32 us
    pallas_call x1, Pallas kernels, gather_rows(): pl.pallas_call(gather_kernel, out_shape=jax.ShapeDtypeStruct((2, 256, 8,...  27.4 us
    pallas_call x1, Pallas kernels, similar_call(): pl.pallas_call(similar_kernel, grid=(count,), out_shape=(jax.ShapeDtypeSt...  16.2 us
    unnamed x10, local copies, waits for them, and re-layouts  4.79 us

profile of v2, /device:TPU:1, one launch (start us, length us, event | category | flops | bytes accessed | tf_op | source)
XLA Modules:
  0.0 123.2 jit_solution(15242578916952796268)
XLA Ops:
  0.6 2.2 %pick_rows.1 = (bf16[2,8,128]{2,1,0:T(8,128)(2,1)}, s32[2,256]{1,0:T(2,128)}) custom-call(s32[2,256]{1,0:T(2,128)} %pivots_ref.1, bf16[3072,1024]{1,0:T(8,128)(2,1)} %emb_ref.3), custom_call_target="tpu_custom_call" | custom-call | tf_op jit(solution)/shard_map/pick_rows/pallas_call | solution.py:518
  2.9 27.4 %gather_rows.1.rows_ref = bf16[2,256,8,128]{3,2,1,0:T(8,128)(2,1)} custom-call(bf16[2,8,128]{2,1,0:T(8,128)(2,1)} %get-tuple-element.12.mine_ref), custom_call_target="tpu_custom_call" | custom-call | tf_op jit(solution)/shard_map/gather_rows/pallas_call | solution.py:180
  30.3 16.2 %similar.1 = (bf16[3072,512]{1,0:T(8,128)(2,1)}, bf16[3072,512]{1,0:T(8,128)(2,1)}, f32[10,128,128]{2,1,0:T(8,128)}, f32[512,512]{1,0:T(8,128)}, f32[1,512]{1,0:T(1,128)}) custom-call(s32[2,256]{1,0:T(2,128)} %get-tuple-element.11.targets_ref, bf16[2,256,8,128]{3,2,1,0:T(8,128)(2,1)} %gather_rows.1.rows_ref, bf16[3072,1024]{1,0:T(8,128)(2,1)} %emb_ref.3), custom_call_target="tpu_custom_call" | custom-call | tf_op jit(solution)/shard_map/similar/pallas_call | solution.py:262
  46.5 0.0 copy-start.1
  46.5 1.2 copy-done.1
  47.7 0.0 copy-start.2
  47.7 1.1 copy-done.2
  48.8 0.0 copy-start.4
  48.8 0.7 copy-done.4
  49.4 39.9 %reduce_gram.1 = (f32[1280,128]{1,0:T(8,128)S(1)}, f32[512,512]{1,0:T(8,128)S(1)}) custom-call(f32[1280,128]{1,0:T(8,128)S(1)} %bitcast.2, f32[512,512]{1,0:T(8,128)S(1)} %copy-done.1, f32[1,512]{1,0:T(1,128)S(1)} %copy-done.4), custom_call_target="tpu_custom_call" | custom-call | tf_op jit(solution)/shard_map/reduce_gram/pallas_call | solution.py:414
  89.4 0.0 copy-start
  89.4 1.0 copy-done
  90.4 0.0 copy-start.3
  90.4 0.8 copy-done.3
  91.2 32.0 %basis.1 = (f32[3072,512]{1,0:T(8,128)}, f32[512,512]{1,0:T(8,128)}) custom-call(f32[10,128,128]{2,1,0:T(8,128)} %bitcast.3, f32[512,512]{1,0:T(8,128)} %copy-done, bf16[3072,512]{1,0:T(8,128)(2,1)} %get-tuple-element.18.high_ref, bf16[3072,512]{1,0:T(8,128)(2,1)} %get-tuple-element.19.low_ref), custom_call_target="tpu_custom_call" | custom-call | tf_op jit(solution)/shard_map/basis/pallas_call | solution.py:474
Async XLA Ops:
  46.5 1.2 copy-start.1
  47.7 1.1 copy-start.2
  48.8 0.7 copy-start.4
  89.4 1.0 copy-start
  90.4 0.8 copy-start.3

commit v3 on v2

--- a/solution.py
+++ b/solution.py
@@ -26,25 +26,37 @@
     count = NB // 8
     rows = list(rows)
     sub = lax.broadcasted_iota(jnp.int32, (8, 128), 0)
+    lane = lax.broadcasted_iota(jnp.int32, (8, 128), 1)
     full = lambda v: jnp.broadcast_to(v, (8, 128))
+
+    def fetch(k):
+        spread = lambda v, j: full(jnp.sum(jnp.where(lane == j, v, 0.0), axis=1, keepdims=True))
+        return {t: [spread(rows[t], 8 * k + c) for c in range(8)] for t in range(k, count)}
+
     out = []
+    now = fetch(0)
     for k in range(count):
-        cols = [[full(rows[t][:, 8 * k + c : 8 * k + c + 1]) for c in range(8)] for t in range(k, count)]
+        later = fetch(k + 1) if k + 1 < count else None
         scale = jnp.zeros((8, 128), F32)
         for c in range(8):
-            pivot = full(cols[0][c][c : c + 1, :])
+            pivot = full(now[k][c][c : c + 1, :])
             pivot_row = full(rows[k][c : c + 1, :])
-            ahead = [full(cols[0][e][c : c + 1, :]) for e in range(c + 1, 8)]
+            ahead = [full(now[k][e][c : c + 1, :]) for e in range(c + 1, 8)]
+            if later is not None:
+                beyond = [full(now[k + 1][c][e : e + 1, :]) for e in range(8)]
             inverse = 1.0 / pivot
             scale = jnp.where(sub == c, pivot, scale)
             for t in range(k, count):
-                mult = cols[t - k][c] * inverse
-                if t == k:
-                    mult = jnp.where(sub > c, mult, 0.0)
+                column = jnp.where(sub > c, now[t][c], 0.0) if t == k else now[t][c]
+                mult = column * inverse
                 rows[t] = rows[t] - mult * pivot_row
                 for e in range(c + 1, 8):
-                    cols[t - k][e] = cols[t - k][e] - mult * ahead[e - c - 1]
+                    now[t][e] = now[t][e] - mult * ahead[e - c - 1]
+                if t > k:
+                    for e in range(8):
+                        later[t][e] = later[t][e] - mult * beyond[e]
         out.append(rows[k] * lax.rsqrt(scale))
+        now = later
     return out
 
 
@@ -52,32 +64,35 @@
     n = w_ref.shape[0]
     lane = lax.broadcasted_iota(jnp.int32, (8, 128), 1)
     sub = lax.broadcasted_iota(jnp.int32, (8, 128), 0)
+    block = w_ref[0:NB, 0:128]
     for k in range(n // NB):
-        r0 = k * NB
-        left = (r0 // 128) * 128
+        r0, r1 = k * NB, k * NB + NB
         rows = []
         for t in range(NB // 8):
-            block = w_ref[r0 + 8 * t : r0 + 8 * t + 8, left : left + 128]
-            if r0 % 128:
-                block = pltpu.roll(block, 64, 1)
-            rows.append(jnp.where(lane < 64, block, jnp.where(lane - 64 == sub + 8 * t, 1.0, 0.0)))
+            eye = jnp.where(lane - NB == sub + 8 * t, 1.0, 0.0)
+            rows.append(jnp.where(lane < NB, block[8 * t : 8 * t + 8, :], eye))
         both = jnp.concatenate(base_block(rows), axis=0)
         diag_ref[k] = both
+        inverse = both[:, NB:]
+        if r1 < n:
+            left = (r1 // 128) * 128
+            ahead, block = w_ref[r0:r1, left : left + 128], w_ref[r1 : r1 + NB, left : left + 128]
+            if r1 % 128:
+                ahead, block = pltpu.roll(ahead, NB, 1), pltpu.roll(block, NB, 1)
+            ahead = dot(inverse, ahead, (1, 0), HI)
+            block = block - dot(ahead[:, :NB], ahead, (0, 0), HI)
         yield
-        wide = w_ref[r0 : r0 + NB, :]
+        wide = w_ref[r0:r1, :]
         col = lax.broadcasted_iota(jnp.int32, (NB, n), 1)
         row = lax.broadcasted_iota(jnp.int32, (NB, n), 0)
-        wide = jnp.where((col >= r0) & (col < r0 + NB), jnp.where(col - r0 == row, 1.0, 0.0), wide)
-        strip = dot(both[:, 64:], wide, (1, 0), HI)
-        w_ref[r0 : r0 + NB, :] = strip
-        if r0 + NB < n:
-            rest = n - r0 - NB
-            update = dot(strip[:, r0 + NB :], strip, (0, 0), HI)
-            current = w_ref[r0 + NB :, :]
-            col = lax.broadcasted_iota(jnp.int32, (rest, n), 1)
-            current = jnp.where((col >= r0) & (col < r0 + NB), 0.0, current)
-            w_ref[r0 + NB :, :] = current - update
-        yield
+        wide = jnp.where((col >= r0) & (col < r1), jnp.where(col - r0 == row, 1.0, 0.0), wide)
+        strip = dot(inverse, wide, (1, 0), HI)
+        w_ref[r0:r1, :] = strip
+        if r1 < n:
+            update = dot(strip[:, r1:], strip, (0, 0), HI)
+            current = w_ref[r1:, :]
+            col = lax.broadcasted_iota(jnp.int32, (n - r1, n), 1)
+            w_ref[r1:, :] = jnp.where((col >= r0) & (col < r1), 0.0, current) - update
 
 
 def cholesky_inverse(w_ref, diag_ref):
@@ -124,8 +139,8 @@
     other = (lax.axis_index("bank"), 1 - core)
     along_x, along_y, along_z = axis_peers(x, y, z, core)
     half = NX * NY * NZ
-    slot_a = core * half + (y * NZ + z) * NX + x
-    slot_b = core * half + (x * NZ + z) * NY + y
+    slot_a = core * half + (y * NX + x) * NZ + z
+    slot_b = core * half + (x * NY + y) * NZ + z
     local = pltpu.make_async_copy(mine_ref.at[0], out_ref.at[0, slot_a], send.at[0])
     local_b = pltpu.make_async_copy(mine_ref.at[1], out_ref.at[1, slot_b], send.at[1])
     local.start()
@@ -149,20 +164,20 @@
         return copies
 
     base = core * half
-    first_a = push(0, base + (y * NZ + z) * NX + x, 1, along_x)
-    first_b = push(1, base + (x * NZ + z) * NY + y, 1, along_y)
+    first_a = push(0, slot_a, 1, along_z)
+    first_b = push(1, slot_b, 1, along_z)
     for copy in first_a:
         copy.wait_recv()
-    second_a = push(0, base + (y * NZ + z) * NX, NX, along_z)
+    second_a = push(0, slot_a - z, NZ, along_x)
     for copy in first_b:
         copy.wait_recv()
-    second_b = push(1, base + (x * NZ + z) * NY, NY, along_z)
+    second_b = push(1, slot_b - z, NZ, along_y)
     for copy in second_a:
         copy.wait_recv()
-    third_a = push(0, base + y * NZ * NX, NZ * NX, along_y)
+    third_a = push(0, base + y * NX * NZ, NX * NZ, along_y)
     for copy in second_b:
         copy.wait_recv()
-    third_b = push(1, base + x * NZ * NY, NZ * NY, along_x)
+    third_b = push(1, base + x * NY * NZ, NY * NZ, along_x)
     for copy in third_a:
         copy.wait_recv()
     last_a = push(0, base, half, [other])
@@ -183,7 +198,7 @@
         in_specs=[pl.BlockSpec(memory_space=pltpu.VMEM)],
         out_specs=pl.BlockSpec(memory_space=pltpu.VMEM),
         scratch_shapes=[pltpu.SemaphoreType.DMA((copies,)), pltpu.SemaphoreType.DMA((copies,))],
-        compiler_params=pltpu.CompilerParams(collective_id=0, has_side_effects=True),
+        compiler_params=pltpu.CompilerParams(collective_id=0, has_side_effects=True, vmem_limit_bytes=8 << 20),
         name="gather_rows",
     )(mine)
 
@@ -277,7 +292,7 @@
             pltpu.VMEM((1, 512), F32),
             pltpu.VMEM((1, 512), F32),
         ],
-        compiler_params=pltpu.CompilerParams(vmem_limit_bytes=56 << 20, dimension_semantics=("arbitrary",)),
+        compiler_params=pltpu.CompilerParams(vmem_limit_bytes=24 << 20, dimension_semantics=("arbitrary",)),
         name="similar",
     )(targets, rows, embeddings)
 
@@ -314,7 +329,7 @@
     big = []
     for s, (start, size) in enumerate(STREAMS):
         peers, n, pos = axes[s]
-        next(work)
+        next(work, None)
         state[s].wait_recv()
         half_sum[pl.ds(start, size), :] = in_ref[pl.ds(mine + start, size), :] + core_in[pl.ds(start, size), :]
         part = size // 4
@@ -334,7 +349,7 @@
         _, n, pos = axes[s]
         peers, n2, pos2 = axes[1 - s]
         part = size // 4
-        next(work)
+        next(work, None)
         for copy in big[s]:
             copy.wait_recv()
         total = half_sum[pl.ds(start + pos * part, part), :]
@@ -357,7 +372,7 @@
     for s, (start, size) in enumerate(STREAMS):
         _, n2, pos2 = axes[1 - s]
         tiny = size // 16
-        next(work)
+        next(work, None)
         for copy in small[s]:
             copy.wait_recv()
         total = big_sum[pl.ds(start // 4 + pos2 * tiny, tiny), :]
@@ -372,7 +387,7 @@
         _, n, pos = axes[s]
         peers, n2, pos2 = axes[1 - s]
         part, tiny = size // 4, size // 16
-        next(work)
+        next(work, None)
         for copy in last[s]:
             copy.wait_recv()
         total = z_in[0, start // 16 : start // 16 + tiny, :]
@@ -386,14 +401,14 @@
     for s, (start, size) in enumerate(STREAMS):
         peers, n, pos = axes[s]
         part = size // 4
-        next(work)
+        next(work, None)
         for copy in back[s]:
             copy.wait_recv()
         piece = out_ref.at[pl.ds(mine + start + pos * part, part)]
         far.append([push(piece, piece, peer) for peer in peers])
     final = []
     for s, (start, size) in enumerate(STREAMS):
-        next(work)
+        next(work, None)
         for copy in far[s]:
             copy.wait_recv()
         piece = out_ref.at[pl.ds(mine + start, size)]
@@ -429,7 +444,7 @@
             pltpu.SemaphoreType.DMA((copies,)),
             pltpu.SemaphoreType.DMA((copies,)),
         ],
-        compiler_params=pltpu.CompilerParams(collective_id=1, has_side_effects=True, vmem_limit_bytes=48 << 20),
+        compiler_params=pltpu.CompilerParams(collective_id=1, has_side_effects=True, vmem_limit_bytes=24 << 20),
         name="reduce_gram",
     )(gram.reshape(1280, 128), block, ratio)
     return total.reshape(10, 128, 128), tail
@@ -483,7 +498,7 @@
             pltpu.VMEM((512, 512), BF16),
             pltpu.VMEM((512, 512), BF16),
         ],
-        compiler_params=pltpu.CompilerParams(vmem_limit_bytes=56 << 20, dimension_semantics=("arbitrary",)),
+        compiler_params=pltpu.CompilerParams(vmem_limit_bytes=24 << 20, dimension_semantics=("arbitrary",)),
         name="basis",
     )(gram, tail, high, low)
 
@@ -503,8 +518,8 @@
     owner = jnp.floor((pivots.astype(F32) + 0.5) * (1.0 / row_count)).astype(jnp.int32)
     bank, core = owner >> 1, owner & 1
     bx, bz, by = bank & (NX - 1), (bank >> 2) & (NZ - 1), bank >> 5
-    first = core * 128 + bank
-    second = core * 128 + (bx * NZ + bz) * NY + by
+    first = core * 128 + (by * NX + bx) * NZ + bz
+    second = core * 128 + (bx * NY + by) * NZ + bz
     targets_ref[...] = jnp.where(lax.broadcasted_iota(jnp.int32, (2, 256), 0) == 0, first, second)
     for s in range(2):
         copies[s].wait()

time: 124 us -> 107 us (0.86)
  Pallas kernels: 118 us -> 102 us
    pallas_call x1, Pallas kernels: 32 us -> 23.8 us  [basis_call(): pl.pallas_call(functools.partial(basis_kernel, total_rows), grid=(count,)...]
    pallas_call x1, Pallas kernels: 16.2 us -> 13.1 us  [similar_call(): pl.pallas_call(similar_kernel, grid=(count,), out_shape=(jax.ShapeDtypeSt...]
    pallas_call x1, Pallas kernels: 39.9 us -> 37.5 us  [reduce_gram(): pl.pallas_call(reduce_kernel, out_shape=(jax.ShapeDtypeStruct((1280, 128)...]
    pallas_call x1, Pallas kernels: 27.4 us -> 25.3 us  [gather_rows(): pl.pallas_call(gather_kernel, out_shape=jax.ShapeDtypeStruct((2, 256, 8,...]
    unnamed x10 -> x6, local copies, waits for them, and re-layouts: 4.79 us -> 4.14 us
where the time goes in v3:
time: 107 us
  Pallas kernels  102 us (95%)
  local copies, waits for them, and re-layouts  4.14 us (4%)
    pallas_call x1, Pallas kernels, reduce_gram(): pl.pallas_call(reduce_kernel, out_shape=(jax.ShapeDtypeStruct((1280, 128)...  37.5 us
    pallas_call x1, Pallas kernels, gather_rows(): pl.pallas_call(gather_kernel, out_shape=jax.ShapeDtypeStruct((2, 256, 8,...  25.3 us
    pallas_call x1, Pallas kernels, basis_call(): pl.pallas_call(functools.partial(basis_kernel, total_rows), grid=(count,)...  23.8 us
    pallas_call x1, Pallas kernels, similar_call(): pl.pallas_call(similar_kernel, grid=(count,), out_shape=(jax.ShapeDtypeSt...  13.1 us
    unnamed x6, local copies, waits for them, and re-layouts  4.14 us
    pallas_call x1, Pallas kernels, pick_rows(): pl.pallas_call(functools.partial(pick_kernel, embeddings.shape[0]), out_s...  2.23 us

profile of v3, /device:TPU:1, one launch (start us, length us, event | category | flops | bytes accessed | tf_op | source)
XLA Modules:
  0.0 106.7 jit_solution(4570093322847313740)
XLA Ops:
  0.6 2.2 %pick_rows.1 = (bf16[2,8,128]{2,1,0:T(8,128)(2,1)}, s32[2,256]{1,0:T(2,128)}) custom-call(s32[2,256]{1,0:T(2,128)} %pivots_ref.1, bf16[3072,1024]{1,0:T(8,128)(2,1)} %emb_ref.3), custom_call_target="tpu_custom_call" | custom-call | tf_op jit(solution)/shard_map/pick_rows/pallas_call | solution.py:533
  2.9 0.0 copy-start.1
  2.9 0.7 copy-done.1
  3.6 25.3 %gather_rows.1.rows_ref = bf16[2,256,8,128]{3,2,1,0:T(8,128)(2,1)S(1)} custom-call(bf16[2,8,128]{2,1,0:T(8,128)(2,1)S(1)} %copy-done.1), custom_call_target="tpu_custom_call" | custom-call | tf_op jit(solution)/shard_map/gather_rows/pallas_call | solution.py:195
  28.9 0.0 copy-start
  28.9 2.8 %copy-done = bf16[3072,1024]{1,0:T(8,128)(2,1)S(1)} copy-done((bf16[3072,1024]{1,0:T(8,128)(2,1)S(1)}, bf16[3072,1024]{1,0:T(8,128)(2,1)}, u32[]{:S(2)}) %copy-start) | copy-done | bytes 6291480
  31.7 0.0 copy-start.2
  31.7 0.7 copy-done.2
  32.3 13.1 %similar.1 = (bf16[3072,512]{1,0:T(8,128)(2,1)S(1)}, bf16[3072,512]{1,0:T(8,128)(2,1)S(1)}, f32[10,128,128]{2,1,0:T(8,128)S(1)}, f32[512,512]{1,0:T(8,128)S(1)}, f32[1,512]{1,0:T(1,128)S(1)}) custom-call(s32[2,256]{1,0:T(2,128)S(1)} %copy-done.2, bf16[2,256,8,128]{3,2,1,0:T(8,128)(2,1)S(1)} %gather_rows.1.rows_ref, bf16[3072,1024]{1,0:T(8,128)(2,1)S(1)} %copy-done), custom_call_target="tpu_custom_call" | custom-call | tf_op jit(solution)/shard_map/similar/pallas_call | solution.py:277
  45.4 37.5 %reduce_gram.1 = (f32[1280,128]{1,0:T(8,128)S(1)}, f32[512,512]{1,0:T(8,128)S(1)}) custom-call(f32[1280,128]{1,0:T(8,128)S(1)} %bitcast.2, f32[512,512]{1,0:T(8,128)S(1)} %get-tuple-element.14.block_ref, f32[1,512]{1,0:T(1,128)S(1)} %get-tuple-element.15.r_ref), custom_call_target="tpu_custom_call" | custom-call | tf_op jit(solution)/shard_map/reduce_gram/pallas_call | solution.py:429
  82.9 23.8 %basis.1 = (f32[3072,512]{1,0:T(8,128)}, f32[512,512]{1,0:T(8,128)}) custom-call(f32[10,128,128]{2,1,0:T(8,128)S(1)} %bitcast.3, f32[512,512]{1,0:T(8,128)S(1)} %get-tuple-element.17.tail_ref, bf16[3072,512]{1,0:T(8,128)(2,1)S(1)} %get-tuple-element.18.high_ref, bf16[3072,512]{1,0:T(8,128)(2,1)S(1)} %get-tuple-element.19.low_ref), custom_call_target="tpu_custom_call" | custom-call | tf_op jit(solution)/shard_map/basis/pallas_call | solution.py:489
Async XLA Ops:
  2.9 0.7 copy-start.1
  28.9 2.8 %copy-start = (bf16[3072,1024]{1,0:T(8,128)(2,1)S(1)}, bf16[3072,1024]{1,0:T(8,128)(2,1)}, u32[]{:S(2)}) copy-start(bf16[3072,1024]{1,0:T(8,128)(2,1)} %emb_ref.3) | copy-start | bytes 18874372
  31.7 0.7 copy-start.2

commit v4 on v3

v4 whole, which is shorter than its diff:
```python
import functools

import jax
import jax.numpy as jnp
from jax import lax
from jax.experimental import pallas as pl
from jax.experimental.pallas import tpu as pltpu
from jax.sharding import PartitionSpec as P

HI = lax.Precision.HIGHEST
F32 = jnp.float32
BF16 = jnp.bfloat16
P_SIZE = 256
NX, NY, NZ = 4, 4, 8
NB = 64
TILE = 512
UPPER = [(i, j) for i in range(4) for j in range(i, 4)]
MESH = pl.DeviceIdType.MESH


def dot(a, b, dims, precision=None):
    return lax.dot_general(a, b, ((dims[:1], dims[1:]), ((), ())), precision=precision, preferred_element_type=F32)


def base_block(rows):
    count = NB // 8
    rows = list(rows)
    sub = lax.broadcasted_iota(jnp.int32, (8, 128), 0)
    lane = lax.broadcasted_iota(jnp.int32, (8, 128), 1)
    full = lambda v: jnp.broadcast_to(v, (8, 128))

    def fetch(k):
        spread = lambda v, j: full(jnp.sum(jnp.where(lane == j, v, 0.0), axis=1, keepdims=True))
        return {t: [spread(rows[t], 8 * k + c) for c in range(8)] for t in range(k, count)}

    out = []
    now = fetch(0)
    for k in range(count):
        later = fetch(k + 1) if k + 1 < count else None
        scale = jnp.zeros((8, 128), F32)
        for c in range(8):
            pivot = full(now[k][c][c : c + 1, :])
            pivot_row = full(rows[k][c : c + 1, :])
            ahead = [full(now[k][e][c : c + 1, :]) for e in range(c + 1, 8)]
            if later is not None:
                beyond = [full(now[k + 1][c][e : e + 1, :]) for e in range(8)]
            inverse = 1.0 / pivot
            scale = jnp.where(sub == c, pivot, scale)
            for t in range(k, count):
                column = jnp.where(sub > c, now[t][c], 0.0) if t == k else now[t][c]
                mult = column * inverse
                rows[t] = rows[t] - mult * pivot_row
                for e in range(c + 1, 8):
                    now[t][e] = now[t][e] - mult * ahead[e - c - 1]
                if t > k:
                    for e in range(8):
                        later[t][e] = later[t][e] - mult * beyond[e]
        out.append(rows[k] * lax.rsqrt(scale))
        now = later
    return out


def cholesky_steps(w_ref, diag_ref):
    n = w_ref.shape[0]
    lane = lax.broadcasted_iota(jnp.int32, (8, 128), 1)
    sub = lax.broadcasted_iota(jnp.int32, (8, 128), 0)
    block = w_ref[0:NB, 0:128]
    for k in range(n // NB):
        r0, r1 = k * NB, k * NB + NB
        rows = []
        for t in range(NB // 8):
            eye = jnp.where(lane - NB == sub + 8 * t, 1.0, 0.0)
            rows.append(jnp.where(lane < NB, block[8 * t : 8 * t + 8, :], eye))
        both = jnp.concatenate(base_block(rows), axis=0)
        diag_ref[k] = both
        inverse = both[:, NB:]
        if r1 < n:
            left = (r1 // 128) * 128
            ahead, block = w_ref[r0:r1, left : left + 128], w_ref[r1 : r1 + NB, left : left + 128]
            if r1 % 128:
                ahead, block = pltpu.roll(ahead, NB, 1), pltpu.roll(block, NB, 1)
            ahead = dot(inverse, ahead, (1, 0), HI)
            block = block - dot(ahead[:, :NB], ahead, (0, 0), HI)
        yield
        wide = w_ref[r0:r1, :]
        col = lax.broadcasted_iota(jnp.int32, (NB, n), 1)
        row = lax.broadcasted_iota(jnp.int32, (NB, n), 0)
        wide = jnp.where((col >= r0) & (col < r1), jnp.where(col - r0 == row, 1.0, 0.0), wide)
        strip = dot(inverse, wide, (1, 0), HI)
        w_ref[r0:r1, :] = strip
        if r1 < n:
            update = dot(strip[:, r1:], strip, (0, 0), HI)
            current = w_ref[r1:, :]
            col = lax.broadcasted_iota(jnp.int32, (n - r1, n), 1)
            w_ref[r1:, :] = jnp.where((col >= r0) & (col < r1), 0.0, current) - update


def cholesky_inverse(w_ref, diag_ref):
    for _ in cholesky_steps(w_ref, diag_ref):
        pass


def lower_blocks(w):
    n = w.shape[0]
    row = lax.broadcasted_iota(jnp.int32, (n, n), 0)
    col = lax.broadcasted_iota(jnp.int32, (n, n), 1)
    return jnp.where(row >= col, w, 0.0)


def coords():
    bank = lax.axis_index("bank")
    core = lax.axis_index("sub")
    x = lax.rem(bank, NX)
    z = lax.rem(bank // NX, NZ)
    y = bank // (NX * NZ)
    return x, y, z, core


def bank_of(x, y, z):
    return (y * NZ + z) * NX + x


def axis_peers(x, y, z, core):
    along_x = [(bank_of(lax.rem(x + o, NX), y, z), core) for o in range(1, NX)]
    along_y = [(bank_of(x, lax.rem(y + o, NY), z), core) for o in range(1, NY)]
    along_z = [(bank_of(x, y, lax.rem(z + o, NZ)), core) for o in range(1, NZ)]
    return along_x, along_y, along_z


LEAD = 16
STREAMS = ((0, 384), (384, 256))


def split(v):
    high = v.astype(BF16)
    return high, (v - high.astype(F32)).astype(BF16)


def gram_kernel(
    mine_hbm, targets_hbm, emb_hbm, high_hbm, low_hbm, out_ref, tail_ref,
    high_ref, low_ref, targets_ref, emb_ref, norms_ref, rows_ref, wide_ref, chosen_ref, norm_ref, r_ref, own_ref, in_ref, w_ref, diag_ref,
    core_in, big_in, small_in, z_in, half_sum, big_sum, small_sum, load, send, recv,
):
    x, y, z, core = coords()
    other = (lax.axis_index("bank"), 1 - core)
    along_x, along_y, along_z = axis_peers(x, y, z, core)
    row_count = emb_hbm.shape[0]
    tiles = row_count // TILE
    everything = []
    count = [2]

    def push(src, dst, peer):
        i = count[0]
        count[0] += 1
        copy = pltpu.make_async_remote_copy(
            src_ref=src, dst_ref=dst, send_sem=send.at[i], recv_sem=recv.at[i], device_id=peer, device_id_type=MESH
        )
        copy.start()
        everything.append(copy)
        return copy

    def arrive(copies):
        for copy in copies:
            copy.wait_recv()

    half = NX * NY * NZ
    base = core * half
    slot_a = base + (y * NX + x) * NZ + z
    slot_b = base + (x * NY + y) * NZ + z
    loads = [
        pltpu.make_async_copy(emb_hbm.at[pl.ds(t * TILE, TILE)], emb_ref.at[pl.ds(t * TILE, TILE)], load.at[t])
        for t in range(tiles)
    ]
    local = [
        pltpu.make_async_copy(mine_hbm.at[0], rows_ref.at[0, slot_a], send.at[0]),
        pltpu.make_async_copy(mine_hbm.at[1], rows_ref.at[1, slot_b], send.at[1]),
        pltpu.make_async_copy(targets_hbm, targets_ref, load.at[tiles]),
    ]
    for copy in local + loads:
        copy.start()
    peers = [other] + along_x + along_y + along_z
    barrier = pltpu.get_barrier_semaphore()
    for peer in peers:
        pl.semaphore_signal(barrier, inc=1, device_id=peer, device_id_type=MESH)

    def norms(first, last):
        for t in range(first, last):
            loads[t].wait()

        def body(i, carry):
            at = pl.ds(pl.multiple_of(i * 64, 64), 64)
            wide = emb_ref[at, :].astype(F32)
            norms_ref[at, :] = jnp.sum(wide * wide, axis=1, keepdims=True)
            return carry

        lax.fori_loop(first * (TILE // 64), last * (TILE // 64), body, 0)

    def share(step, start, size, to):
        part = rows_ref.at[step, pl.ds(start, size)]
        return [push(part, part, peer) for peer in to]

    for copy in local:
        copy.wait()
    pl.semaphore_wait(barrier, len(peers))
    first_a = share(0, slot_a, 1, along_z)
    first_b = share(1, slot_b, 1, along_z)
    norms(0, 2)
    arrive(first_a)
    second_a = share(0, slot_a - z, NZ, along_x)
    arrive(first_b)
    second_b = share(1, slot_b - z, NZ, along_y)
    norms(2, 4)
    arrive(second_a)
    third_a = share(0, base + y * NX * NZ, NX * NZ, along_y)
    arrive(second_b)
    third_b = share(1, base + x * NY * NZ, NY * NZ, along_x)
    norms(4, tiles)
    arrive(third_a)
    last_a = share(0, base, half, [other])
    arrive(third_b)
    last_b = share(1, base, half, [other])

    for s, copies in ((0, last_a), (1, last_b)):
        slot = lax.broadcasted_iota(jnp.int32, (256, 256), 0)
        pick = jnp.where(slot == targets_ref[s : s + 1, :], 1.0, 0.0).astype(BF16)
        arrive(copies)
        wide_ref[...] = rows_ref[s].reshape(2048, 128).astype(F32)
        for q in range(8):
            part = wide_ref[pl.ds(q, 256, stride=8), :].astype(BF16)
            chosen_ref[256 * s : 256 * s + 256, 128 * q : 128 * q + 128] = dot(pick, part, (0, 0)).astype(BF16)
    dots = dot(chosen_ref[...], chosen_ref[...], (1, 1))
    row = lax.broadcasted_iota(jnp.int32, (512, 512), 0)
    col = lax.broadcasted_iota(jnp.int32, (512, 512), 1)
    own = jnp.where(row == col, dots, 0.0)
    norm_row = jnp.sum(own, axis=0, keepdims=True)
    norm_ref[...] = norm_row
    block = dots / (jnp.sum(own, axis=1, keepdims=True) + norm_row - dots)
    w_ref[...] = block
    lead = jnp.sum(jnp.where(col < LEAD, block, 0.0), axis=1, keepdims=True) * (1.0 / LEAD)
    use = (row >= LEAD) & (row != col)
    above = jnp.sum(jnp.where(use, block * lead, 0.0), axis=0, keepdims=True)
    below = jnp.sum(jnp.where(use, lead * lead, 0.0), axis=0, keepdims=True)
    ratio = above / jnp.where(below > 0.0, below, 1.0)
    ratio = jnp.where(below > 0.0, jnp.clip(ratio, -4.0, 4.0), 0.0)
    r_ref[...] = jnp.where(lax.broadcasted_iota(jnp.int32, (1, 512), 1) < LEAD, 0.0, ratio)
    in_ref[...] = jnp.zeros_like(in_ref)
    own_ref[...] = jnp.zeros_like(own_ref)

    def tile(t, carry):
        at = pl.ds(pl.multiple_of(t * TILE, TILE), TILE)
        dots = dot(emb_ref[at, :], chosen_ref[...], (1, 1))
        similar = dots / (norms_ref[at, :] + norm_ref[...] - dots)
        lane = lax.broadcasted_iota(jnp.int32, (TILE, 128), 1)
        lead = jnp.sum(jnp.where(lane < LEAD, similar[:, :128], 0.0), axis=1, keepdims=True) * (1.0 / LEAD)
        similar = similar - lead * r_ref[...]
        high, low = split(similar)
        high_ref[at, :] = high
        low_ref[at, :] = low
        own_ref[...] += jnp.sum(low.astype(F32) * low.astype(F32), axis=0, keepdims=True)
        for b, (i, j) in enumerate(UPPER):
            if i == j:
                left_high, left_low = high[:, 128 * i : 128 * i + 128], low[:, 128 * i : 128 * i + 128]
                part = dot(left_high, high[:, 128 * i :], (0, 0))
                part += dot(left_high, low[:, 128 * i :], (0, 0)) + dot(left_low, high[:, 128 * i :], (0, 0))
                for e in range(4 - i):
                    in_ref[128 * (b + e) : 128 * (b + e) + 128, :] += part[:, 128 * e : 128 * e + 128]
        return carry

    lax.fori_loop(0, tiles, tile, 0)
    row = lax.broadcasted_iota(jnp.int32, (128, 128), 0)
    col = lax.broadcasted_iota(jnp.int32, (128, 128), 1)
    for b, (i, j) in enumerate(UPPER):
        if i == j:
            in_ref[128 * b : 128 * b + 128, :] += jnp.where(row == col, own_ref[:, 128 * i : 128 * i + 128], 0.0)

    work = cholesky_steps(w_ref, diag_ref)
    mine = core * 640
    theirs = (1 - core) * 640
    axes = ((along_x, NX, x), (along_y, NY, y))
    state = [
        push(in_ref.at[pl.ds(theirs + start, size)], core_in.at[pl.ds(start, size)], other) for start, size in STREAMS
    ]
    stores = [
        pltpu.make_async_copy(high_ref, high_hbm, load.at[tiles + 1]),
        pltpu.make_async_copy(low_ref, low_hbm, load.at[tiles + 2]),
    ]
    for copy in stores:
        copy.start()
    big = []
    for s, (start, size) in enumerate(STREAMS):
        peers, n, pos = axes[s]
        state[s].wait_recv()
        half_sum[pl.ds(start, size), :] = in_ref[pl.ds(mine + start, size), :] + core_in[pl.ds(start, size), :]
        part = size // 4
        copies = []
        for o in range(1, n):
            to = lax.rem(pos + o, n)
            piece = half_sum.at[pl.ds(start + to * part, part)]
            copies.append(push(piece, big_in.at[o - 1, pl.ds(start // 4, part)], peers[o - 1]))
        big.append(copies)
    next(work)
    next(work)
    small = []
    for s, (start, size) in enumerate(STREAMS):
        _, n, pos = axes[s]
        peers, n2, pos2 = axes[1 - s]
        part = size // 4
        arrive(big[s])
        total = half_sum[pl.ds(start + pos * part, part), :]
        for o in range(n - 1):
            total = total + big_in[o, start // 4 : start // 4 + part, :]
        big_sum[start // 4 : start // 4 + part, :] = total
        tiny = part // 4
        copies = []
        for o in range(1, n2):
            to = lax.rem(pos2 + o, n2)
            piece = big_sum.at[pl.ds(start // 4 + to * tiny, tiny)]
            copies.append(push(piece, small_in.at[o - 1, pl.ds(start // 16, tiny)], peers[o - 1]))
        small.append(copies)
    next(work)
    last = []
    for s, (start, size) in enumerate(STREAMS):
        _, n2, pos2 = axes[1 - s]
        tiny = size // 16
        arrive(small[s])
        total = big_sum[pl.ds(start // 4 + pos2 * tiny, tiny), :]
        for o in range(n2 - 1):
            total = total + small_in[o, start // 16 : start // 16 + tiny, :]
        small_sum[start // 16 : start // 16 + tiny, :] = total
        piece = small_sum.at[pl.ds(start // 16, tiny)]
        last.append([push(piece, z_in.at[z, pl.ds(start // 16, tiny)], peer) for peer in along_z])
        z_in[z, start // 16 : start // 16 + tiny, :] = total
    next(work)
    next(work)
    back = []
    for s, (start, size) in enumerate(STREAMS):
        _, n, pos = axes[s]
        peers, n2, pos2 = axes[1 - s]
        part, tiny = size // 4, size // 16
        arrive(last[s])
        total = z_in[0, start // 16 : start // 16 + tiny, :]
        for o in range(1, NZ):
            total = total + z_in[o, start // 16 : start // 16 + tiny, :]
        at = mine + start + pos * part + pos2 * tiny
        out_ref[pl.ds(at, tiny), :] = total
        piece = out_ref.at[pl.ds(at, tiny)]
        back.append([push(piece, piece, peer) for peer in peers])
    next(work)
    far = []
    for s, (start, size) in enumerate(STREAMS):
        peers, n, pos = axes[s]
        part = size // 4
        arrive(back[s])
        piece = out_ref.at[pl.ds(mine + start + pos * part, part)]
        far.append([push(piece, piece, peer) for peer in peers])
    for _ in work:
        pass
    final = []
    for s, (start, size) in enumerate(STREAMS):
        arrive(far[s])
        piece = out_ref.at[pl.ds(mine + start, size)]
        final.append(push(piece, piece, other))
    inverse = lower_blocks(w_ref[...])
    weight = jnp.sum(inverse * r_ref[...], axis=1, keepdims=True) * (1.0 / LEAD)
    tail_ref[...] = inverse + jnp.where(lax.broadcasted_iota(jnp.int32, (512, 512), 1) < LEAD, weight, 0.0)
    arrive(final)
    for copy in stores:
        copy.wait()
    for copy in everything:
        copy.wait_send()


def gram_call(mine, targets, embeddings):
    rows = embeddings.shape[0]
    copies = 2 + 2 * (7 + 3 + 3 + 1) + 2 * (1 + 3 + 3 + 7 + 3 + 3 + 1)
    vmem = pl.BlockSpec(memory_space=pltpu.VMEM)
    return pl.pallas_call(
        gram_kernel,
        out_shape=(
            jax.ShapeDtypeStruct((rows, 512), BF16),
            jax.ShapeDtypeStruct((rows, 512), BF16),
            jax.ShapeDtypeStruct((1280, 128), F32),
            jax.ShapeDtypeStruct((512, 512), F32),
        ),
        in_specs=[pl.BlockSpec(memory_space=pltpu.HBM)] * 3,
        out_specs=(pl.BlockSpec(memory_space=pltpu.HBM),) * 2 + (vmem,) * 2,
        scratch_shapes=[
            pltpu.VMEM((rows, 512), BF16),
            pltpu.VMEM((rows, 512), BF16),
            pltpu.VMEM((2, 256), jnp.int32),
            pltpu.VMEM((rows, 1024), BF16),
            pltpu.VMEM((rows, 1), F32),
            pltpu.VMEM((2, 256, 8, 128), BF16),
            pltpu.VMEM((2048, 128), F32),
            pltpu.VMEM((512, 1024), BF16),
            pltpu.VMEM((1, 512), F32),
            pltpu.VMEM((1, 512), F32),
            pltpu.VMEM((1, 512), F32),
            pltpu.VMEM((1280, 128), F32),
            pltpu.VMEM((512, 512), F32),
            pltpu.VMEM((8, NB, 128), F32),
            pltpu.VMEM((640, 128), F32),
            pltpu.VMEM((3, 160, 128), F32),
            pltpu.VMEM((3, 40, 128), F32),
            pltpu.VMEM((NZ, 40, 128), F32),
            pltpu.VMEM((640, 128), F32),
            pltpu.VMEM((160, 128), F32),
            pltpu.VMEM((40, 128), F32),
            pltpu.SemaphoreType.DMA((rows // TILE + 3,)),
            pltpu.SemaphoreType.DMA((copies,)),
            pltpu.SemaphoreType.DMA((copies,)),
        ],
        compiler_params=pltpu.CompilerParams(collective_id=0, has_side_effects=True, vmem_limit_bytes=52 << 20),
        name="gram",
    )(mine, targets, embeddings)


def basis_kernel(total_rows, gram_ref, tail_ref, high_ref, low_ref, basis_ref, triangle_ref, w_ref, diag_ref, inv_high, inv_low):
    @pl.when(pl.program_id(0) == 0)
    def _():
        for b, (i, j) in enumerate(UPPER):
            w_ref[128 * i : 128 * i + 128, 128 * j : 128 * j + 128] = gram_ref[b] / total_rows
        cholesky_inverse(w_ref, diag_ref)
        w = w_ref[...]
        inv_high[...], inv_low[...] = split(lower_blocks(w))
        row = lax.broadcasted_iota(jnp.int32, (512, 512), 0)
        col = lax.broadcasted_iota(jnp.int32, (512, 512), 1)
        w_ref[...] = jnp.where(row < col, w, 0.0)
        lane = lax.broadcasted_iota(jnp.int32, (NB, 128), 1)
        sub = lax.broadcasted_iota(jnp.int32, (NB, 128), 0)
        for k in range(8):
            left = 128 * (k // 2)
            both = diag_ref[k]
            keep = w_ref[NB * k : NB * k + NB, left : left + 128]
            if k % 2:
                mine = pltpu.roll(both, 64, 1)
                keep = jnp.where(lane >= 64, jnp.where(lane - 64 >= sub, mine, 0.0), keep)
            else:
                keep = jnp.where(lane < 64, jnp.where(lane >= sub, both, 0.0), keep)
            w_ref[NB * k : NB * k + NB, left : left + 128] = keep
        triangle_ref[...] = dot(w_ref[...], tail_ref[...], (1, 1), HI)

    high, low = high_ref[...], low_ref[...]
    for start, depth in ((0, 256), (256, 512)):
        right_high, right_low = inv_high[start : start + 256, :depth], inv_low[start : start + 256, :depth]
        out = dot(low[:, :depth], right_high, (1, 1)) + dot(high[:, :depth], right_low, (1, 1))
        basis_ref[:, start : start + 256] = out + dot(high[:, :depth], right_high, (1, 1))


def basis_call(gram, tail, high, low, total_rows):
    count = high.shape[0] // TILE
    whole = lambda shape: pl.BlockSpec(shape, lambda i: (0,) * len(shape))
    tile = pl.BlockSpec((TILE, 512), lambda i: (i, 0))
    return pl.pallas_call(
        functools.partial(basis_kernel, total_rows),
        grid=(count,),
        out_shape=(jax.ShapeDtypeStruct(high.shape, F32), jax.ShapeDtypeStruct((512, 512), F32)),
        in_specs=[whole((10, 128, 128)), whole((512, 512)), tile, tile],
        out_specs=(tile, whole((512, 512))),
        scratch_shapes=[
            pltpu.VMEM((512, 512), F32),
            pltpu.VMEM((8, NB, 128), F32),
            pltpu.VMEM((512, 512), BF16),
            pltpu.VMEM((512, 512), BF16),
        ],
        compiler_params=pltpu.CompilerParams(vmem_limit_bytes=52 << 20, dimension_semantics=("arbitrary",)),
        name="basis",
    )(gram, tail, high, low)


def pick_kernel(row_count, pivots_ref, emb_ref, mine_ref, targets_ref, block_ref, sems):
    start = (lax.axis_index("bank") * 2 + lax.axis_index("sub")) * row_count
    pivots = pivots_ref[...]
    inside = (pivots >= start) & (pivots < start + row_count)
    copies, offsets = [], []
    for s in range(2):
        local = jnp.sum(jnp.where(inside[s : s + 1], pivots[s : s + 1] - start, 0))
        first = pl.multiple_of((local // 16) * 16, 16)
        copy = pltpu.make_async_copy(emb_ref.at[pl.ds(first, 16)], block_ref.at[s], sems.at[s])
        copy.start()
        copies.append(copy)
        offsets.append(local - first)
    owner = jnp.floor((pivots.astype(F32) + 0.5) * (1.0 / row_count)).astype(jnp.int32)
    bank, core = owner >> 1, owner & 1
    bx, bz, by = bank & (NX - 1), (bank >> 2) & (NZ - 1), bank >> 5
    first = core * 128 + (by * NX + bx) * NZ + bz
    second = core * 128 + (bx * NY + by) * NZ + bz
    targets_ref[...] = jnp.where(lax.broadcasted_iota(jnp.int32, (2, 256), 0) == 0, first, second)
    for s in range(2):
        copies[s].wait()
        rows = block_ref[s].astype(F32)
        keep = lax.broadcasted_iota(jnp.int32, (16, 1024), 0) == offsets[s]
        row = jnp.sum(jnp.where(keep, rows, 0.0), axis=0, keepdims=True)
        mine_ref[s] = jnp.concatenate([row[:, 128 * q : 128 * q + 128] for q in range(8)], axis=0).astype(BF16)


def pick_rows(pivots, embeddings):
    return pl.pallas_call(
        functools.partial(pick_kernel, embeddings.shape[0]),
        out_shape=(jax.ShapeDtypeStruct((2, 8, 128), BF16), jax.ShapeDtypeStruct((2, 256), jnp.int32)),
        in_specs=[pl.BlockSpec(memory_space=pltpu.VMEM), pl.BlockSpec(memory_space=pl.ANY)],
        out_specs=(pl.BlockSpec(memory_space=pltpu.VMEM),) * 2,
        scratch_shapes=[pltpu.VMEM((2, 16, 1024), BF16), pltpu.SemaphoreType.DMA((2,))],
        compiler_params=pltpu.CompilerParams(vmem_limit_bytes=52 << 20),
        name="pick_rows",
    )(pivots, embeddings)


def per_device(embeddings, pivots):
    total_rows = embeddings.shape[0] * lax.axis_size(("bank", "sub"))
    mine, targets = pick_rows(pivots, embeddings)
    high, low, gram, tail = gram_call(mine, targets, embeddings)
    gram = gram.reshape(10, 128, 128)
    return basis_call(gram, tail, high, low, float(total_rows))


def solution(mesh):
    in_specs = (P(("bank", "sub"), None), P())
    out_specs = (P(("bank", "sub"), None), P())
    return jax.shard_map(per_device, mesh=mesh, in_specs=in_specs, out_specs=out_specs, check_vma=False)
```

time: 107 us -> 93.9 us (0.88)
  Pallas kernels: 102 us -> 92.2 us
  local copies, waits for them, and re-layouts: 4.14 us -> 0.67 us
    pallas_call x3 -> x1, Pallas kernels: 75.8 us -> 64.8 us  [gram_call(): pl.pallas_call(gram_kernel, out_shape=(jax.ShapeDtypeStruct((rows, 512),...]
    unnamed x6 -> x2, local copies, waits for them, and re-layouts: 4.14 us -> 0.67 us
    pallas_call x1, Pallas kernels: 23.8 us -> 26.4 us  [basis_call(): pl.pallas_call(functools.partial(basis_kernel, total_rows), grid=(count,)...]
    pallas_call x1, Pallas kernels: 2.23 us -> 0.96 us  [pick_rows(): pl.pallas_call(functools.partial(pick_kernel, embeddings.shape[0]), out_s...]
where the time goes in v4:
time: 93.9 us; the launch traced here: 93.5 us
  Pallas kernels  92.2 us (98%)
    pallas_call x1, Pallas kernels, gram_call(): pl.pallas_call(gram_kernel, out_shape=(jax.ShapeDtypeStruct((rows, 512),...  64.8 us
    pallas_call x1, Pallas kernels, basis_call(): pl.pallas_call(functools.partial(basis_kernel, total_rows), grid=(count,)...  26.4 us

profile of v4, /device:TPU:1, one launch (start us, length us, event | category | flops | bytes accessed | tf_op | source)
XLA Modules:
  0.0 93.5 jit_solution(12310746541008483527)
XLA Ops:
  0.6 0.0 copy-start
  0.6 0.7 copy-done
  1.3 1.0 %pick_rows.1 = (bf16[2,8,128]{2,1,0:T(8,128)(2,1)S(1)}, s32[2,256]{1,0:T(2,128)S(1)}) custom-call(s32[2,256]{1,0:T(2,128)S(1)} %copy-done, bf16[3072,1024]{1,0:T(8,128)(2,1)} %emb_hbm.1), custom_call_target="tpu_custom_call" | custom-call | tf_op jit(solution)/shard_map/pick_rows/pallas_call | solution.py:498
  2.3 64.8 %gram.1 = (bf16[3072,512]{1,0:T(8,128)(2,1)}, bf16[3072,512]{1,0:T(8,128)(2,1)}, f32[1280,128]{1,0:T(8,128)S(1)}, f32[512,512]{1,0:T(8,128)S(1)}) custom-call(bf16[2,8,128]{2,1,0:T(8,128)(2,1)S(1)} %get-tuple-element.8.mine_hbm, s32[2,256]{1,0:T(2,128)S(1)} %get-tuple-element.9.targets_hbm, bf16[3072,1024]{1,0:T(8,128)(2,1)} %emb_hbm.1), custom_call_target="tpu_custom_call" | custom-call | tf_op jit(solution)/shard_map/gram/pallas_call | solution.py:377
  67.1 26.4 %basis.1 = (f32[3072,512]{1,0:T(8,128)}, f32[512,512]{1,0:T(8,128)}) custom-call(f32[10,128,128]{2,1,0:T(8,128)S(1)} %bitcast.1, f32[512,512]{1,0:T(8,128)S(1)} %get-tuple-element.11.tail_ref, bf16[3072,512]{1,0:T(8,128)(2,1)} %get-tuple-element.12.high_ref, bf16[3072,512]{1,0:T(8,128)(2,1)} %get-tuple-element.13.low_ref), custom_call_target="tpu_custom_call" | custom-call | tf_op jit(solution)/shard_map/basis/pallas_call | solution.py:454
Async XLA Ops:
  0.6 0.7 copy-start

commit v5 on v4

--- a/solution.py
+++ b/solution.py
@@ -438,7 +438,10 @@
             else:
                 keep = jnp.where(lane < 64, jnp.where(lane >= sub, both, 0.0), keep)
             w_ref[NB * k : NB * k + NB, left : left + 128] = keep
-        triangle_ref[...] = dot(w_ref[...], tail_ref[...], (1, 1), HI)
+        triangle_ref[:256, :256] = dot(w_ref[:256, :256], tail_ref[:256, :256], (1, 1), HI)
+        triangle_ref[:256, 256:] = dot(w_ref[:256, :], tail_ref[256:, :], (1, 1), HI)
+        triangle_ref[256:, 256:] = dot(w_ref[256:, 256:], tail_ref[256:, 256:], (1, 1), HI)
+        triangle_ref[256:, :256] = jnp.zeros((256, 256), F32)
 
     high, low = high_ref[...], low_ref[...]
     for start, depth in ((0, 256), (256, 512)):

time: 93.9 us -> 93 us (level)
  no operation moved by 1% of the time
where the time goes in v5:
time: 93 us; the launch traced here: 92.7 us
  Pallas kernels  91.3 us (98%)
    pallas_call x1, Pallas kernels, gram_call(): pl.pallas_call(gram_kernel, out_shape=(jax.ShapeDtypeStruct((rows, 512),...  64.8 us
    pallas_call x1, Pallas kernels, basis_call(): pl.pallas_call(functools.partial(basis_kernel, total_rows), grid=(count,)...  25.5 us

profile of v5, /device:TPU:1, one launch (start us, length us, event | category | flops | bytes accessed | tf_op | source)
XLA Modules:
  0.0 92.7 jit_solution(16056932373737696451)
XLA Ops:
  0.6 0.0 copy-start
  0.6 0.7 copy-done
  1.3 1.0 %pick_rows.1 = (bf16[2,8,128]{2,1,0:T(8,128)(2,1)S(1)}, s32[2,256]{1,0:T(2,128)S(1)}) custom-call(s32[2,256]{1,0:T(2,128)S(1)} %copy-done, bf16[3072,1024]{1,0:T(8,128)(2,1)} %emb_hbm.1), custom_call_target="tpu_custom_call" | custom-call | tf_op jit(solution)/shard_map/pick_rows/pallas_call | solution.py:501
  2.3 64.8 %gram.1 = (bf16[3072,512]{1,0:T(8,128)(2,1)}, bf16[3072,512]{1,0:T(8,128)(2,1)}, f32[1280,128]{1,0:T(8,128)S(1)}, f32[512,512]{1,0:T(8,128)S(1)}) custom-call(bf16[2,8,128]{2,1,0:T(8,128)(2,1)S(1)} %get-tuple-element.8.mine_hbm, s32[2,256]{1,0:T(2,128)S(1)} %get-tuple-element.9.targets_hbm, bf16[3072,1024]{1,0:T(8,128)(2,1)} %emb_hbm.1), custom_call_target="tpu_custom_call" | custom-call | tf_op jit(solution)/shard_map/gram/pallas_call | solution.py:377
  67.1 25.5 %basis.1 = (f32[3072,512]{1,0:T(8,128)}, f32[512,512]{1,0:T(8,128)}) custom-call(f32[10,128,128]{2,1,0:T(8,128)S(1)} %bitcast.1, f32[512,512]{1,0:T(8,128)S(1)} %get-tuple-element.11.tail_ref, bf16[3072,512]{1,0:T(8,128)(2,1)} %get-tuple-element.12.high_ref, bf16[3072,512]{1,0:T(8,128)(2,1)} %get-tuple-element.13.low_ref), custom_call_target="tpu_custom_call" | custom-call | tf_op jit(solution)/shard_map/basis/pallas_call | solution.py:457
Async XLA Ops:
  0.6 0.7 copy-start
